TPU v7x, 32 devices: a whole 2x2x4 slice. The times are simulated.
32 devices in a mesh: gx: 4 (over y, x), gy: 4 (over z), gz: 2 (over core).
Axes of the slice: x: 2, y: 2, z: 4, core: 2. Of those that a mesh axis runs over, the one named last changes fastest.
Arguments:
- state: float32 [3, 32, 160, 512], P(None, 'gz', 'gy', 'gx'), may hold values from -6 to 6
- right_side: float32 [3, 32, 160, 512], P(None, 'gz', 'gy', 'gx'), may hold values from -6 to 6
- permeability: bfloat16 [32, 160, 512], P('gz', 'gy', 'gx'), may hold values from 0.099609375 to 10
- pore_volume: bfloat16 [32, 160, 512], P('gz', 'gy', 'gx'), may hold values from 0.019897461 to 0.19921875
- facies: int32 [32], P('gz'), may hold values from 0 to 3
- storage_table: float32 [4, 3, 3], replicated, may hold values from -0.3 to 2, as said below
- coupling_table: float32 [4, 3, 3], replicated, may hold values from -0.3 to 2, as said below
Outputs:
- new_state: float32 [3, 32, 160, 512], P(None, 'gz', 'gy', 'gx')
- correction: float32 [160, 512], P('gy', 'gx')
Inputs may be any that keep to these rules, and one draw needn't show every extreme that they name: `storage_table`: each facies block has a diagonal of 1 to 2 and off-diagonal entries of magnitude at most 0.3. `coupling_table`: each facies block has a diagonal of 1 to 2 and off-diagonal entries of magnitude at most 0.3.
All inputs are finite; a program needn't handle non-finite values.
Results may differ from a plain program's by a relative error of at most 0.0003.
Values sent between devices are 32-bit elements; how exact they have to be, the bound alone decides.
A program may use at most 64 MiB of HBM per device.

v0:
```python
import jax
import jax.numpy as jnp
from jax import lax
from jax.sharding import PartitionSpec as P

SWEEPS = 8
relax = 0.8


def extended(cells, sides, width):
    for axis, dim in sides:
        count = lax.axis_size(axis)
        ends = count - 1
        head = lax.slice_in_dim(cells, 0, width, axis=dim)
        tail = lax.slice_in_dim(cells, cells.shape[dim] - width, cells.shape[dim], axis=dim)
        cells = jnp.concatenate(
            [
                lax.ppermute(tail, axis, [(i, (i + 1) % count) for i in range(ends)]),
                cells,
                lax.ppermute(head, axis, [((i + 1) % count, i) for i in range(ends)]),
            ],
            axis=dim,
        )
    return cells


def layer_tables(facies, table):
    onehot = (facies[:, None] == jnp.arange(table.shape[0])[None, :]).astype(jnp.float32)
    return jnp.dot(onehot, table.reshape(table.shape[0], 9), precision=lax.Precision.HIGHEST)


def layer_coefficient(rows, row_index, column_index):
    return rows[:, 3 * row_index + column_index][:, None, None]


def neighbours(padded):
    return [
        padded[..., 2:, 1:-1, 1:-1],
        padded[..., :-2, 1:-1, 1:-1],
        padded[..., 1:-1, 2:, 1:-1],
        padded[..., 1:-1, :-2, 1:-1],
        padded[..., 1:-1, 1:-1, 2:],
        padded[..., 1:-1, 1:-1, :-2],
    ]


def face_weights(padded_perm):
    center = padded_perm[1:-1, 1:-1, 1:-1]
    return [2.0 * center * nearby / (center + nearby) for nearby in neighbours(padded_perm)]


def apply_operator(padded_state, weights, storage, storage_rows, coupling_rows):
    center = padded_state[:, 1:-1, 1:-1, 1:-1]
    fluxes = jnp.zeros_like(center)
    for weight, nearby in zip(weights, neighbours(padded_state)):
        fluxes = fluxes + weight[None] * (center - nearby)
    outputs = []
    for row_index in range(3):
        local = sum((layer_coefficient(storage_rows, row_index, k) * center[k] for k in range(3)))
        moved = sum((layer_coefficient(coupling_rows, row_index, k) * fluxes[k] for k in range(3)))
        outputs.append(storage * local + moved)
    return jnp.stack(outputs)


def coarse_planes(residual, weights, storage, storage_rows, coupling_rows):
    first_coupling = layer_coefficient(coupling_rows, 0, 0)
    first_storage = layer_coefficient(storage_rows, 0, 0)
    items = [residual[0], storage * first_storage] + [
        weights[k] * first_coupling for k in range(2, 6)
    ]
    return jnp.stack([jnp.sum(item, axis=0) for item in items])


def jacobi(field, bordered, planes):
    diagonal = planes[1] + planes[2] + planes[3] + planes[4] + planes[5]
    nearby = (
        planes[2] * bordered[2:, 1:-1]
        + planes[3] * bordered[:-2, 1:-1]
        + planes[4] * bordered[1:-1, 2:]
        + planes[5] * bordered[1:-1, :-2]
    )
    return field + relax * (planes[0] - diagonal * field + nearby) / diagonal


def column_image(correction, bordered, weights, storage, storage_rows, coupling_rows):
    areal = (
        weights[2] * (correction - bordered[2:, 1:-1])
        + weights[3] * (correction - bordered[:-2, 1:-1])
        + weights[4] * (correction - bordered[1:-1, 2:])
        + weights[5] * (correction - bordered[1:-1, :-2])
    )
    return jnp.stack(
        [
            storage * layer_coefficient(storage_rows, r, 0) * correction
            + layer_coefficient(coupling_rows, r, 0) * areal
            for r in range(3)
        ]
    )


def block_solve(weights, storage, storage_rows, coupling_rows, residual):
    face_total = weights[0] + weights[1] + weights[2] + weights[3] + weights[4] + weights[5]
    entries = [
        [
            storage * layer_coefficient(storage_rows, r, c)
            + face_total * layer_coefficient(coupling_rows, r, c)
            for c in range(3)
        ]
        for r in range(3)
    ]

    def cofactor(r, c):
        return (
            entries[(r + 1) % 3][(c + 1) % 3] * entries[(r + 2) % 3][(c + 2) % 3]
            - entries[(r + 1) % 3][(c + 2) % 3] * entries[(r + 2) % 3][(c + 1) % 3]
        )

    factors = [[cofactor(r, c) for c in range(3)] for r in range(3)]
    determinant = (
        entries[0][0] * factors[0][0]
        + entries[0][1] * factors[0][1]
        + entries[0][2] * factors[0][2]
    )
    return jnp.stack(
        [
            (
                factors[0][r] * residual[0]
                + factors[1][r] * residual[1]
                + factors[2][r] * residual[2]
            )
            / determinant
            for r in range(3)
        ]
    )


def per_device(state, right_side, permeability, pore_volume, facies, storage_table, coupling_table):
    perm_wide = permeability.astype(jnp.float32)
    storage = pore_volume.astype(jnp.float32)
    storage_rows = layer_tables(facies, storage_table)
    coupling_rows = layer_tables(facies, coupling_table)
    stacked = jnp.concatenate([state, perm_wide[None]], axis=0)
    padded = extended(stacked, (("gz", 1), ("gy", 2), ("gx", 3)), 1)
    weights = face_weights(padded[3])
    residual = right_side - apply_operator(
        padded[:3], weights, storage, storage_rows, coupling_rows
    )
    planes = coarse_planes(residual, weights, storage, storage_rows, coupling_rows)
    totals = lax.psum(planes, "gz")
    correction = jnp.zeros(totals.shape[1:], jnp.float32)
    for repeat_index in range(SWEEPS):
        bordered = extended(correction, (("gy", 0), ("gx", 1)), 1)
        correction = jacobi(correction, bordered, totals)
    state_one = state.at[0].add(correction[None])
    bordered = extended(correction, (("gy", 0), ("gx", 1)), 1)
    later_residual = residual - column_image(
        correction, bordered, weights, storage, storage_rows, coupling_rows
    )
    new_state = state_one + block_solve(
        weights, storage, storage_rows, coupling_rows, later_residual
    )
    return (new_state, correction)


def solution(mesh):
    return jax.shard_map(
        per_device,
        mesh=mesh,
        in_specs=(
            P(None, "gz", "gy", "gx"),
            P(None, "gz", "gy", "gx"),
            P("gz", "gy", "gx"),
            P("gz", "gy", "gx"),
            P("gz"),
            P(),
            P(),
        ),
        out_specs=(P(None, "gz", "gy", "gx"), P("gy", "gx")),
        check_vma=False,
    )
```

profile of v0, /device:TPU:28, one launch (start us, length us, event | category | flops | bytes accessed | tf_op | source)
XLA Modules:
  0.0 220.8 jit_solution(13019892907075081389)
XLA Ops:
  8.5 2.3 %collective-permute-start.6 = (f32[1,128]{1,0:T(1,128)S(1)}, f32[1,128]{1,0:T(1,128)S(1)}, u32[]{:S(2)}, u32[]{:S(2)}) collective-permute-start(f32[1,128]{1,0:T(1,128)S(1)} %broadcast.60), channel_id=1, source_target_pairs={{2,0},{4,2},{6,4},{3,1},{5,3},{7,5},{10,8},{12,10},{14,12},{11,9},... | collective-permute-start | bytes 1544 | tf_op jit(solution)/shard_map/ppermute | solution.py:20
  10.8 1.3 collective-permute-start.7
  12.2 1.5 collective-permute-start
  13.7 1.3 collective-permute-start.1
  16.9 1.3 collective-permute-start.2
  18.2 5.0 %collective-permute-start.3 = (f32[4,18,1,128]{3,0,2,1:T(4,128)S(1)}, f32[4,18,1,128]{3,0,2,1:T(4,128)S(1)}, u32[]{:S(2)}, u32[]{:S(2)}) collective-permute-start(f32[4,18,1,128]{3,0,2,1:T(4,128)S(1)} %copy.245), channel_id=1, source_target_pairs={{2,0},{4,2},{6,4},{3,1},{5,3},{7,5},{10,8},{12,10},{14,12},{11,9},... | collective-permute-start | bytes 110600 | tf_op jit(solution)/shard_map/ppermute | solution.py:20
  25.2 1.8 fusion.155
  26.9 2.2 copy.218
  29.1 3.4 %collective-permute-start.4 = (f32[4,18,42,1]{2,0,3,1:T(4,128)S(1)}, f32[4,18,42,1]{2,0,3,1:T(4,128)S(1)}, u32[]{:S(2)}, u32[]{:S(2)}) collective-permute-start(f32[4,18,42,1]{2,0,3,1:T(4,128)S(1)} %copy.218), channel_id=1, source_target_pairs={{0,8},{8,16},{16,24},{1,9},{9,17},{17,25},{2,10},{10,18},{18,26},{... | collective-permute-start | bytes 36296 | tf_op jit(solution)/shard_map/ppermute | solution.py:18
  33.2 3.3 %collective-permute-start.5 = (f32[4,18,42,1]{2,0,3,1:T(4,128)S(1)}, f32[4,18,42,1]{2,0,3,1:T(4,128)S(1)}, u32[]{:S(2)}, u32[]{:S(2)}) collective-permute-start(f32[4,18,42,1]{2,0,3,1:T(4,128)S(1)} %copy.219), channel_id=1, source_target_pairs={{8,0},{16,8},{24,16},{9,1},{17,9},{25,17},{10,2},{18,10},{26,18},{... | collective-permute-start | bytes 36296 | tf_op jit(solution)/shard_map/ppermute | solution.py:20
  37.4 1.7 collective-permute-done.5
  39.0 1.9 copy.221
  40.9 1.5 fusion.24
  44.0 3.3 %fusion.2 = f32[3,16,40,128]{3,2,1,0:T(8,128)S(1)} fusion(f32[3,16,40,128]{3,2,1,0:T(8,128)S(1)} %copy.254, f32[4,18,42,1]{3,2,1,0:T(8,128)S(1)} %copy.220, f32[4,18,1,128]{3,2,1,0:T(1,128)S(1)} %copy.217, f32[4,18,1,128]{3,2,1,0:T(1,128)S(1)} %copy.216, f32[4,1,40,128]{3,2,1,0:T(8,128)S(1)} %collective-permute-done.1, ...), kind=kLoop, calls=%fused_computation.18 | loop fusion | flops 10076160 | bytes 4521600 | tf_op jit(solution)/shard_map/add | solution.py:56
  51.7 4.2 %collective-permute-start.8 = (f32[42,1]{1,0:T(8,128)S(1)}, f32[42,1]{1,0:T(8,128)S(1)}, u32[]{:S(2)}, u32[]{:S(2)}) collective-permute-start(f32[42,1]{1,0:T(8,128)S(1)} %get-tuple-element.66), channel_id=1, source_target_pairs={{8,0},{16,8},{24,16},{9,1},{17,9},{25,17},{10,2},{18,10},{26,18},{... | collective-permute-start | bytes 512 | tf_op jit(solution)/shard_map/ppermute | solution.py:20
  56.0 1.9 collective-permute-start.9
  57.9 4.7 %collective-permute-done.9 = f32[42,1]{1,0:T(8,128)S(1)} collective-permute-done((f32[42,1]{1,0:T(8,128)S(1)}, f32[42,1]{1,0:T(8,128)S(1)}, u32[]{:S(2)}, u32[]{:S(2)}) %collective-permute-start.9) | collective-permute-done | bytes 200 | tf_op jit(solution)/shard_map/ppermute | solution.py:18
  62.6 9.7 %all-reduce.4.cloned.1.call-done = f32[6,40,128]{2,1,0:T(8,128)} async-done(((f32[6,40,128]{2,1,0:T(8,128)}), f32[6,40,128]{2,1,0:T(8,128)}) %all-reduce.4.cloned.1.call-update) | async-done | bytes 122896 | tf_op jit(solution)/shard_map/psum | solution.py:149
  73.3 2.4 %collective-permute-start.10 = (f32[1,128]{1,0:T(1,128)S(1)}, f32[1,128]{1,0:T(1,128)S(1)}, u32[]{:S(2)}, u32[]{:S(2)}) collective-permute-start(f32[1,128]{1,0:T(1,128)S(1)} %get-tuple-element.87), channel_id=1, source_target_pairs={{2,0},{4,2},{6,4},{3,1},{5,3},{7,5},{10,8},{12,10},{14,12},{11,9},... | collective-permute-start | bytes 1544 | tf_op jit(solution)/shard_map/ppermute | solution.py:20
  75.8 1.4 collective-permute-start.11
  77.2 4.2 %collective-permute-done.11 = f32[1,128]{1,0:T(1,128)S(1)} collective-permute-done((f32[1,128]{1,0:T(1,128)S(1)}, f32[1,128]{1,0:T(1,128)S(1)}, u32[]{:S(2)}, u32[]{:S(2)}) %collective-permute-start.11) | collective-permute-done | bytes 544 | tf_op jit(solution)/shard_map/ppermute | solution.py:18
  81.4 3.4 %collective-permute-start.12 = (f32[42,1]{1,0:T(8,128)S(1)}, f32[42,1]{1,0:T(8,128)S(1)}, u32[]{:S(2)}, u32[]{:S(2)}) collective-permute-start(f32[42,1]{1,0:T(8,128)S(1)} %get-tuple-element.64), channel_id=1, source_target_pairs={{8,0},{16,8},{24,16},{9,1},{17,9},{25,17},{10,2},{18,10},{26,18},{... | collective-permute-start | bytes 512 | tf_op jit(solution)/shard_map/ppermute | solution.py:20
  84.8 2.5 %collective-permute-start.13 = (f32[42,1]{1,0:T(8,128)S(1)}, f32[42,1]{1,0:T(8,128)S(1)}, u32[]{:S(2)}, u32[]{:S(2)}) collective-permute-start(f32[42,1]{1,0:T(8,128)S(1)} %get-tuple-element.65), channel_id=1, source_target_pairs={{0,8},{8,16},{16,24},{1,9},{9,17},{17,25},{2,10},{10,18},{18,26},{... | collective-permute-start | bytes 512 | tf_op jit(solution)/shard_map/ppermute | solution.py:18
  87.3 4.1 %collective-permute-done.13 = f32[42,1]{1,0:T(8,128)S(1)} collective-permute-done((f32[42,1]{1,0:T(8,128)S(1)}, f32[42,1]{1,0:T(8,128)S(1)}, u32[]{:S(2)}, u32[]{:S(2)}) %collective-permute-start.13) | collective-permute-done | bytes 200 | tf_op jit(solution)/shard_map/ppermute | solution.py:18
  92.3 2.4 %collective-permute-start.14 = (f32[1,128]{1,0:T(1,128)S(1)}, f32[1,128]{1,0:T(1,128)S(1)}, u32[]{:S(2)}, u32[]{:S(2)}) collective-permute-start(f32[1,128]{1,0:T(1,128)S(1)} %get-tuple-element.85), channel_id=1, source_target_pairs={{2,0},{4,2},{6,4},{3,1},{5,3},{7,5},{10,8},{12,10},{14,12},{11,9},... | collective-permute-start | bytes 1544 | tf_op jit(solution)/shard_map/ppermute | solution.py:20
  94.8 1.3 collective-permute-start.15
  96.1 4.2 %collective-permute-done.15 = f32[1,128]{1,0:T(1,128)S(1)} collective-permute-done((f32[1,128]{1,0:T(1,128)S(1)}, f32[1,128]{1,0:T(1,128)S(1)}, u32[]{:S(2)}, u32[]{:S(2)}) %collective-permute-start.15) | collective-permute-done | bytes 544 | tf_op jit(solution)/shard_map/ppermute | solution.py:18
  100.4 1.9 collective-permute-start.16
  102.3 3.9 %collective-permute-start.17 = (f32[42,1]{1,0:T(8,128)S(1)}, f32[42,1]{1,0:T(8,128)S(1)}, u32[]{:S(2)}, u32[]{:S(2)}) collective-permute-start(f32[42,1]{1,0:T(8,128)S(1)} %get-tuple-element.63), channel_id=1, source_target_pairs={{0,8},{8,16},{16,24},{1,9},{9,17},{17,25},{2,10},{10,18},{18,26},{... | collective-permute-start | bytes 512 | tf_op jit(solution)/shard_map/ppermute | solution.py:18
  106.2 2.7 %collective-permute-done.17 = f32[42,1]{1,0:T(8,128)S(1)} collective-permute-done((f32[42,1]{1,0:T(8,128)S(1)}, f32[42,1]{1,0:T(8,128)S(1)}, u32[]{:S(2)}, u32[]{:S(2)}) %collective-permute-start.17) | collective-permute-done | bytes 200 | tf_op jit(solution)/shard_map/ppermute | solution.py:18
  109.8 2.4 %collective-permute-start.18 = (f32[1,128]{1,0:T(1,128)S(1)}, f32[1,128]{1,0:T(1,128)S(1)}, u32[]{:S(2)}, u32[]{:S(2)}) collective-permute-start(f32[1,128]{1,0:T(1,128)S(1)} %get-tuple-element.83), channel_id=1, source_target_pairs={{2,0},{4,2},{6,4},{3,1},{5,3},{7,5},{10,8},{12,10},{14,12},{11,9},... | collective-permute-start | bytes 1544 | tf_op jit(solution)/shard_map/ppermute | solution.py:20
  112.3 1.3 collective-permute-start.19
  113.6 4.2 %collective-permute-done.19 = f32[1,128]{1,0:T(1,128)S(1)} collective-permute-done((f32[1,128]{1,0:T(1,128)S(1)}, f32[1,128]{1,0:T(1,128)S(1)}, u32[]{:S(2)}, u32[]{:S(2)}) %collective-permute-start.19) | collective-permute-done | bytes 544 | tf_op jit(solution)/shard_map/ppermute | solution.py:18
  117.8 1.9 collective-permute-start.20
  119.7 3.9 %collective-permute-start.21 = (f32[42,1]{1,0:T(8,128)S(1)}, f32[42,1]{1,0:T(8,128)S(1)}, u32[]{:S(2)}, u32[]{:S(2)}) collective-permute-start(f32[42,1]{1,0:T(8,128)S(1)} %get-tuple-element.61), channel_id=1, source_target_pairs={{0,8},{8,16},{16,24},{1,9},{9,17},{17,25},{2,10},{10,18},{18,26},{... | collective-permute-start | bytes 512 | tf_op jit(solution)/shard_map/ppermute | solution.py:18
  123.7 2.7 %collective-permute-done.21 = f32[42,1]{1,0:T(8,128)S(1)} collective-permute-done((f32[42,1]{1,0:T(8,128)S(1)}, f32[42,1]{1,0:T(8,128)S(1)}, u32[]{:S(2)}, u32[]{:S(2)}) %collective-permute-start.21) | collective-permute-done | bytes 200 | tf_op jit(solution)/shard_map/ppermute | solution.py:18
  127.3 1.9 collective-permute-start.22
  129.2 1.3 collective-permute-start.23
  130.5 4.2 %collective-permute-done.23 = f32[1,128]{1,0:T(1,128)S(1)} collective-permute-done((f32[1,128]{1,0:T(1,128)S(1)}, f32[1,128]{1,0:T(1,128)S(1)}, u32[]{:S(2)}, u32[]{:S(2)}) %collective-permute-start.23) | collective-permute-done | bytes 544 | tf_op jit(solution)/shard_map/ppermute | solution.py:18
  134.8 1.9 collective-permute-start.24
  136.7 3.9 %collective-permute-start.25 = (f32[42,1]{1,0:T(8,128)S(1)}, f32[42,1]{1,0:T(8,128)S(1)}, u32[]{:S(2)}, u32[]{:S(2)}) collective-permute-start(f32[42,1]{1,0:T(8,128)S(1)} %get-tuple-element.59), channel_id=1, source_target_pairs={{0,8},{8,16},{16,24},{1,9},{9,17},{17,25},{2,10},{10,18},{18,26},{... | collective-permute-start | bytes 512 | tf_op jit(solution)/shard_map/ppermute | solution.py:18
  140.6 2.7 %collective-permute-done.25 = f32[42,1]{1,0:T(8,128)S(1)} collective-permute-done((f32[42,1]{1,0:T(8,128)S(1)}, f32[42,1]{1,0:T(8,128)S(1)}, u32[]{:S(2)}, u32[]{:S(2)}) %collective-permute-start.25) | collective-permute-done | bytes 200 | tf_op jit(solution)/shard_map/ppermute | solution.py:18
  144.2 1.9 collective-permute-start.26
  146.2 1.3 collective-permute-start.27
  147.5 4.2 %collective-permute-done.27 = f32[1,128]{1,0:T(1,128)S(1)} collective-permute-done((f32[1,128]{1,0:T(1,128)S(1)}, f32[1,128]{1,0:T(1,128)S(1)}, u32[]{:S(2)}, u32[]{:S(2)}) %collective-permute-start.27) | collective-permute-done | bytes 544 | tf_op jit(solution)/shard_map/ppermute | solution.py:18
  151.7 1.9 collective-permute-start.28
  153.6 3.9 %collective-permute-start.29 = (f32[42,1]{1,0:T(8,128)S(1)}, f32[42,1]{1,0:T(8,128)S(1)}, u32[]{:S(2)}, u32[]{:S(2)}) collective-permute-start(f32[42,1]{1,0:T(8,128)S(1)} %get-tuple-element.57), channel_id=1, source_target_pairs={{0,8},{8,16},{16,24},{1,9},{9,17},{17,25},{2,10},{10,18},{18,26},{... | collective-permute-start | bytes 512 | tf_op jit(solution)/shard_map/ppermute | solution.py:18
  157.6 2.7 %collective-permute-done.29 = f32[42,1]{1,0:T(8,128)S(1)} collective-permute-done((f32[42,1]{1,0:T(8,128)S(1)}, f32[42,1]{1,0:T(8,128)S(1)}, u32[]{:S(2)}, u32[]{:S(2)}) %collective-permute-start.29) | collective-permute-done | bytes 200 | tf_op jit(solution)/shard_map/ppermute | solution.py:18
  160.4 1.9 collective-permute-start.30
  162.3 1.3 collective-permute-start.31
  163.6 4.2 %collective-permute-done.31 = f32[1,128]{1,0:T(1,128)S(1)} collective-permute-done((f32[1,128]{1,0:T(1,128)S(1)}, f32[1,128]{1,0:T(1,128)S(1)}, u32[]{:S(2)}, u32[]{:S(2)}) %collective-permute-start.31) | collective-permute-done | bytes 544 | tf_op jit(solution)/shard_map/ppermute | solution.py:18
  167.8 1.9 collective-permute-start.32
  169.7 3.9 %collective-permute-start.33 = (f32[42,1]{1,0:T(8,128)S(1)}, f32[42,1]{1,0:T(8,128)S(1)}, u32[]{:S(2)}, u32[]{:S(2)}) collective-permute-start(f32[42,1]{1,0:T(8,128)S(1)} %get-tuple-element.55), channel_id=1, source_target_pairs={{0,8},{8,16},{16,24},{1,9},{9,17},{17,25},{2,10},{10,18},{18,26},{... | collective-permute-start | bytes 512 | tf_op jit(solution)/shard_map/ppermute | solution.py:18
  173.7 2.7 %collective-permute-done.33 = f32[42,1]{1,0:T(8,128)S(1)} collective-permute-done((f32[42,1]{1,0:T(8,128)S(1)}, f32[42,1]{1,0:T(8,128)S(1)}, u32[]{:S(2)}, u32[]{:S(2)}) %collective-permute-start.33) | collective-permute-done | bytes 200 | tf_op jit(solution)/shard_map/ppermute | solution.py:18
  176.5 2.0 collective-permute-start.34
  179.9 4.2 %collective-permute-done.35 = f32[1,128]{1,0:T(1,128)S(1)} collective-permute-done((f32[1,128]{1,0:T(1,128)S(1)}, f32[1,128]{1,0:T(1,128)S(1)}, u32[]{:S(2)}, u32[]{:S(2)}) %collective-permute-start.35) | collective-permute-done | bytes 544 | tf_op jit(solution)/shard_map/ppermute | solution.py:18
  184.1 1.9 collective-permute-start.36
  186.1 3.9 %collective-permute-start.37 = (f32[42,1]{1,0:T(8,128)S(1)}, f32[42,1]{1,0:T(8,128)S(1)}, u32[]{:S(2)}, u32[]{:S(2)}) collective-permute-start(f32[42,1]{1,0:T(8,128)S(1)} %get-tuple-element.53), channel_id=1, source_target_pairs={{0,8},{8,16},{16,24},{1,9},{9,17},{17,25},{2,10},{10,18},{18,26},{... | collective-permute-start | bytes 512 | tf_op jit(solution)/shard_map/ppermute | solution.py:18
  190.0 2.7 %collective-permute-done.37 = f32[42,1]{1,0:T(8,128)S(1)} collective-permute-done((f32[42,1]{1,0:T(8,128)S(1)}, f32[42,1]{1,0:T(8,128)S(1)}, u32[]{:S(2)}, u32[]{:S(2)}) %collective-permute-start.37) | collective-permute-done | bytes 200 | tf_op jit(solution)/shard_map/ppermute | solution.py:18
  192.8 1.9 collective-permute-start.38
  196.0 4.2 %collective-permute-done.39 = f32[1,128]{1,0:T(1,128)S(1)} collective-permute-done((f32[1,128]{1,0:T(1,128)S(1)}, f32[1,128]{1,0:T(1,128)S(1)}, u32[]{:S(2)}, u32[]{:S(2)}) %collective-permute-start.39) | collective-permute-done | bytes 544 | tf_op jit(solution)/shard_map/ppermute | solution.py:18
  200.3 1.9 collective-permute-start.40
  202.2 4.1 %collective-permute-start.41 = (f32[42,1]{1,0:T(8,128)S(1)}, f32[42,1]{1,0:T(8,128)S(1)}, u32[]{:S(2)}, u32[]{:S(2)}) collective-permute-start(f32[42,1]{1,0:T(8,128)S(1)} %get-tuple-element.51), channel_id=1, source_target_pairs={{0,8},{8,16},{16,24},{1,9},{9,17},{17,25},{2,10},{10,18},{18,26},{... | collective-permute-start | bytes 512 | tf_op jit(solution)/shard_map/ppermute | solution.py:18
  206.4 2.5 %collective-permute-done.41 = f32[42,1]{1,0:T(8,128)S(1)} collective-permute-done((f32[42,1]{1,0:T(8,128)S(1)}, f32[42,1]{1,0:T(8,128)S(1)}, u32[]{:S(2)}, u32[]{:S(2)}) %collective-permute-start.41) | collective-permute-done | bytes 200 | tf_op jit(solution)/shard_map/ppermute | solution.py:18
  (216 shorter events, 25.4 us)
Async XLA Ops:
  7.2 5.0 %copy-start.18 = (bf16[16,40,128]{2,1,0:T(8,128)(2,1)S(1)}, bf16[16,40,128]{2,1,0:T(8,128)(2,1)}, u32[]{:S(2)}) copy-start(bf16[16,40,128]{2,1,0:T(8,128)(2,1)} %param.11) | copy-start | bytes 491524
  7.2 8.0 %copy-start.49 = (s32[16]{0:T(128)S(1)}, s32[16]{0:T(128)}, u32[]{:S(2)}) copy-start(s32[16]{0:T(128)} %param.13) | copy-start | bytes 196
  7.2 7.9 %copy-start.44 = (f32[4,3,3]{2,0,1:T(4,128)S(1)}, f32[4,3,3]{2,0,1:T(4,128)}, u32[]{:S(2)}) copy-start(f32[4,3,3]{2,0,1:T(4,128)} %param.14) | copy-start | bytes 436
  7.2 7.8 %copy-start.43 = (f32[4,3,3]{2,0,1:T(4,128)S(1)}, f32[4,3,3]{2,0,1:T(4,128)}, u32[]{:S(2)}) copy-start(f32[4,3,3]{2,0,1:T(4,128)} %param.15) | copy-start | bytes 436
  7.2 65.1 %all-reduce.4.cloned.1.call-start = ((), (), s32[]{:S(2)}) async-start(), calls=%async_computation | async-start | bytes 245760 | tf_op jit(solution)/shard_map/psum | solution.py:149
  8.5 28.1 %collective-permute-start.6 = (f32[1,128]{1,0:T(1,128)S(1)}, f32[1,128]{1,0:T(1,128)S(1)}, u32[]{:S(2)}, u32[]{:S(2)}) collective-permute-start(f32[1,128]{1,0:T(1,128)S(1)} %broadcast.60), channel_id=1, source_target_pairs={{2,0},{4,2},{6,4},{3,1},{5,3},{7,5},{10,8},{12,10},{14,12},{11,9},... | collective-permute-start | bytes 1544 | tf_op jit(solution)/shard_map/ppermute | solution.py:20
  10.8 25.7 %collective-permute-start.7 = (f32[1,128]{1,0:T(1,128)S(1)}, f32[1,128]{1,0:T(1,128)S(1)}, u32[]{:S(2)}, u32[]{:S(2)}) collective-permute-start(f32[1,128]{1,0:T(1,128)S(1)} %broadcast.60), channel_id=1, source_target_pairs={{0,2},{2,4},{4,6},{1,3},{3,5},{5,7},{8,10},{10,12},{12,14},{9,11},... | collective-permute-start | bytes 1544 | tf_op jit(solution)/shard_map/ppermute | solution.py:18
  12.2 4.0 %collective-permute-start = (f32[4,1,40,128]{3,2,1,0:T(8,128)S(1)}, f32[4,1,40,128]{3,2,1,0:T(8,128)S(1)}, u32[]{:S(2)}, u32[]{:S(2)}) collective-permute-start(f32[4,1,40,128]{3,2,1,0:T(8,128)S(1)} %get-tuple-element.34), channel_id=1, source_target_pairs={{0,1},{2,3},{4,5},{6,7},{8,9},{10,11},{12,13},{14,15},{16,17},{18,... | collective-permute-start | bytes 245768 | tf_op jit(solution)/shard_map/ppermute | solution.py:18
  13.7 3.2 %collective-permute-start.1 = (f32[4,1,40,128]{3,2,1,0:T(8,128)S(1)}, f32[4,1,40,128]{3,2,1,0:T(8,128)S(1)}, u32[]{:S(2)}, u32[]{:S(2)}) collective-permute-start(f32[4,1,40,128]{3,2,1,0:T(8,128)S(1)} %get-tuple-element.35), channel_id=1, source_target_pairs={{1,0},{3,2},{5,4},{7,6},{9,8},{11,10},{13,12},{15,14},{17,16},{19,... | collective-permute-start | bytes 245768 | tf_op jit(solution)/shard_map/ppermute | solution.py:20
  16.9 6.9 %collective-permute-start.2 = (f32[4,18,1,128]{3,0,2,1:T(4,128)S(1)}, f32[4,18,1,128]{3,0,2,1:T(4,128)S(1)}, u32[]{:S(2)}, u32[]{:S(2)}) collective-permute-start(f32[4,18,1,128]{3,0,2,1:T(4,128)S(1)} %copy.244), channel_id=1, source_target_pairs={{0,2},{2,4},{4,6},{1,3},{3,5},{5,7},{8,10},{10,12},{12,14},{9,11},... | collective-permute-start | bytes 110600 | tf_op jit(solution)/shard_map/ppermute | solution.py:18
  18.2 6.6 %collective-permute-start.3 = (f32[4,18,1,128]{3,0,2,1:T(4,128)S(1)}, f32[4,18,1,128]{3,0,2,1:T(4,128)S(1)}, u32[]{:S(2)}, u32[]{:S(2)}) collective-permute-start(f32[4,18,1,128]{3,0,2,1:T(4,128)S(1)} %copy.245), channel_id=1, source_target_pairs={{2,0},{4,2},{6,4},{3,1},{5,3},{7,5},{10,8},{12,10},{14,12},{11,9},... | collective-permute-start | bytes 110600 | tf_op jit(solution)/shard_map/ppermute | solution.py:20
  29.1 7.5 %collective-permute-start.4 = (f32[4,18,42,1]{2,0,3,1:T(4,128)S(1)}, f32[4,18,42,1]{2,0,3,1:T(4,128)S(1)}, u32[]{:S(2)}, u32[]{:S(2)}) collective-permute-start(f32[4,18,42,1]{2,0,3,1:T(4,128)S(1)} %copy.218), channel_id=1, source_target_pairs={{0,8},{8,16},{16,24},{1,9},{9,17},{17,25},{2,10},{10,18},{18,26},{... | collective-permute-start | bytes 36296 | tf_op jit(solution)/shard_map/ppermute | solution.py:18
  33.2 5.8 %collective-permute-start.5 = (f32[4,18,42,1]{2,0,3,1:T(4,128)S(1)}, f32[4,18,42,1]{2,0,3,1:T(4,128)S(1)}, u32[]{:S(2)}, u32[]{:S(2)}) collective-permute-start(f32[4,18,42,1]{2,0,3,1:T(4,128)S(1)} %copy.219), channel_id=1, source_target_pairs={{8,0},{16,8},{24,16},{9,1},{17,9},{25,17},{10,2},{18,10},{26,18},{... | collective-permute-start | bytes 36296 | tf_op jit(solution)/shard_map/ppermute | solution.py:20
  36.6 4.4 %copy-start.45 = (f32[1,128]{1,0:T(1,128)}, f32[1,128]{1,0:T(1,128)S(1)}, u32[]{:S(2)}) copy-start(f32[1,128]{1,0:T(1,128)S(1)} %collective-permute-done.6) | copy-start | bytes 1540
  36.6 4.4 %copy-start.47 = (f32[1,128]{1,0:T(1,128)}, f32[1,128]{1,0:T(1,128)S(1)}, u32[]{:S(2)}) copy-start(f32[1,128]{1,0:T(1,128)S(1)} %collective-permute-done.7) | copy-start | bytes 1540
  43.7 3.6 %copy-start.3 = (f32[16,40,128]{2,1,0:T(8,128)}, f32[16,40,128]{2,1,0:T(8,128)S(1)}, u32[]{:S(2)}) copy-start(f32[16,40,128]{2,1,0:T(8,128)S(1)} %get-tuple-element.39) | copy-start | bytes 983044
  43.7 3.6 %copy-start.5 = (f32[16,40,128]{2,1,0:T(8,128)}, f32[16,40,128]{2,1,0:T(8,128)S(1)}, u32[]{:S(2)}) copy-start(f32[16,40,128]{2,1,0:T(8,128)S(1)} %get-tuple-element.41) | copy-start | bytes 983044
  43.7 3.6 %copy-start.7 = (f32[16,40,128]{2,1,0:T(8,128)}, f32[16,40,128]{2,1,0:T(8,128)S(1)}, u32[]{:S(2)}) copy-start(f32[16,40,128]{2,1,0:T(8,128)S(1)} %get-tuple-element.43) | copy-start | bytes 983044
  43.7 3.6 %copy-start.9 = (f32[16,40,128]{2,1,0:T(8,128)}, f32[16,40,128]{2,1,0:T(8,128)S(1)}, u32[]{:S(2)}) copy-start(f32[16,40,128]{2,1,0:T(8,128)S(1)} %get-tuple-element.45) | copy-start | bytes 983044
  43.7 3.6 %copy-start.12 = (f32[16,40,128]{2,1,0:T(8,128)}, f32[16,40,128]{2,1,0:T(8,128)S(1)}, u32[]{:S(2)}) copy-start(f32[16,40,128]{2,1,0:T(8,128)S(1)} %get-tuple-element.36) | copy-start | bytes 983044
  43.7 3.6 %copy-start.14 = (f32[16,40,128]{2,1,0:T(8,128)}, f32[16,40,128]{2,1,0:T(8,128)S(1)}, u32[]{:S(2)}) copy-start(f32[16,40,128]{2,1,0:T(8,128)S(1)} %get-tuple-element.37) | copy-start | bytes 983044
  49.5 22.8 %copy-start.46 = (f32[1,128]{1,0:T(1,128)S(1)}, f32[1,128]{1,0:T(1,128)}, u32[]{:S(2)}) copy-start(f32[1,128]{1,0:T(1,128)} %copy-done.45) | copy-start | bytes 1540
  49.5 22.8 %copy-start.48 = (f32[1,128]{1,0:T(1,128)S(1)}, f32[1,128]{1,0:T(1,128)}, u32[]{:S(2)}) copy-start(f32[1,128]{1,0:T(1,128)} %copy-done.47) | copy-start | bytes 1540
  51.7 6.2 %collective-permute-start.8 = (f32[42,1]{1,0:T(8,128)S(1)}, f32[42,1]{1,0:T(8,128)S(1)}, u32[]{:S(2)}, u32[]{:S(2)}) collective-permute-start(f32[42,1]{1,0:T(8,128)S(1)} %get-tuple-element.66), channel_id=1, source_target_pairs={{8,0},{16,8},{24,16},{9,1},{17,9},{25,17},{10,2},{18,10},{26,18},{... | collective-permute-start | bytes 512 | tf_op jit(solution)/shard_map/ppermute | solution.py:20
  56.0 6.6 %collective-permute-start.9 = (f32[42,1]{1,0:T(8,128)S(1)}, f32[42,1]{1,0:T(8,128)S(1)}, u32[]{:S(2)}, u32[]{:S(2)}) collective-permute-start(f32[42,1]{1,0:T(8,128)S(1)} %get-tuple-element.67), channel_id=1, source_target_pairs={{0,8},{8,16},{16,24},{1,9},{9,17},{17,25},{2,10},{10,18},{18,26},{... | collective-permute-start | bytes 512 | tf_op jit(solution)/shard_map/ppermute | solution.py:18
  72.3 87.9 %copy-start.2 = (f32[6,40,128]{2,1,0:T(8,128)S(1)}, f32[6,40,128]{2,1,0:T(8,128)}, u32[]{:S(2)}) copy-start(f32[6,40,128]{2,1,0:T(8,128)} %all-reduce.4.cloned.1.call-done) | copy-start | bytes 368644
  73.3 3.9 %collective-permute-start.10 = (f32[1,128]{1,0:T(1,128)S(1)}, f32[1,128]{1,0:T(1,128)S(1)}, u32[]{:S(2)}, u32[]{:S(2)}) collective-permute-start(f32[1,128]{1,0:T(1,128)S(1)} %get-tuple-element.87), channel_id=1, source_target_pairs={{2,0},{4,2},{6,4},{3,1},{5,3},{7,5},{10,8},{12,10},{14,12},{11,9},... | collective-permute-start | bytes 1544 | tf_op jit(solution)/shard_map/ppermute | solution.py:20
  75.7 133.2 %copy-start.4 = (f32[16,40,128]{2,1,0:T(8,128)S(1)}, f32[16,40,128]{2,1,0:T(8,128)}, u32[]{:S(2)}) copy-start(f32[16,40,128]{2,1,0:T(8,128)} %copy-done.3) | copy-start | bytes 983044
  75.7 133.2 %copy-start.6 = (f32[16,40,128]{2,1,0:T(8,128)S(1)}, f32[16,40,128]{2,1,0:T(8,128)}, u32[]{:S(2)}) copy-start(f32[16,40,128]{2,1,0:T(8,128)} %copy-done.5) | copy-start | bytes 983044
  75.7 133.2 %copy-start.8 = (f32[16,40,128]{2,1,0:T(8,128)S(1)}, f32[16,40,128]{2,1,0:T(8,128)}, u32[]{:S(2)}) copy-start(f32[16,40,128]{2,1,0:T(8,128)} %copy-done.7) | copy-start | bytes 983044
  75.7 133.2 %copy-start.10 = (f32[16,40,128]{2,1,0:T(8,128)S(1)}, f32[16,40,128]{2,1,0:T(8,128)}, u32[]{:S(2)}) copy-start(f32[16,40,128]{2,1,0:T(8,128)} %copy-done.9) | copy-start | bytes 983044
  75.7 133.2 %copy-start.26 = (f32[16]{0:T(128)S(1)}, f32[16]{0:T(128)}, u32[]{:S(2)}) copy-start(f32[16]{0:T(128)} %get-tuple-element.88) | copy-start | bytes 196
  75.8 5.6 %collective-permute-start.11 = (f32[1,128]{1,0:T(1,128)S(1)}, f32[1,128]{1,0:T(1,128)S(1)}, u32[]{:S(2)}, u32[]{:S(2)}) collective-permute-start(f32[1,128]{1,0:T(1,128)S(1)} %get-tuple-element.86), channel_id=1, source_target_pairs={{0,2},{2,4},{4,6},{1,3},{3,5},{5,7},{8,10},{10,12},{12,14},{9,11},... | collective-permute-start | bytes 1544 | tf_op jit(solution)/shard_map/ppermute | solution.py:18
  81.4 5.8 %collective-permute-start.12 = (f32[42,1]{1,0:T(8,128)S(1)}, f32[42,1]{1,0:T(8,128)S(1)}, u32[]{:S(2)}, u32[]{:S(2)}) collective-permute-start(f32[42,1]{1,0:T(8,128)S(1)} %get-tuple-element.64), channel_id=1, source_target_pairs={{8,0},{16,8},{24,16},{9,1},{17,9},{25,17},{10,2},{18,10},{26,18},{... | collective-permute-start | bytes 512 | tf_op jit(solution)/shard_map/ppermute | solution.py:20
  84.8 6.6 %collective-permute-start.13 = (f32[42,1]{1,0:T(8,128)S(1)}, f32[42,1]{1,0:T(8,128)S(1)}, u32[]{:S(2)}, u32[]{:S(2)}) collective-permute-start(f32[42,1]{1,0:T(8,128)S(1)} %get-tuple-element.65), channel_id=1, source_target_pairs={{0,8},{8,16},{16,24},{1,9},{9,17},{17,25},{2,10},{10,18},{18,26},{... | collective-permute-start | bytes 512 | tf_op jit(solution)/shard_map/ppermute | solution.py:18
  92.3 3.8 %collective-permute-start.14 = (f32[1,128]{1,0:T(1,128)S(1)}, f32[1,128]{1,0:T(1,128)S(1)}, u32[]{:S(2)}, u32[]{:S(2)}) collective-permute-start(f32[1,128]{1,0:T(1,128)S(1)} %get-tuple-element.85), channel_id=1, source_target_pairs={{2,0},{4,2},{6,4},{3,1},{5,3},{7,5},{10,8},{12,10},{14,12},{11,9},... | collective-permute-start | bytes 1544 | tf_op jit(solution)/shard_map/ppermute | solution.py:20
  94.8 5.5 %collective-permute-start.15 = (f32[1,128]{1,0:T(1,128)S(1)}, f32[1,128]{1,0:T(1,128)S(1)}, u32[]{:S(2)}, u32[]{:S(2)}) collective-permute-start(f32[1,128]{1,0:T(1,128)S(1)} %get-tuple-element.84), channel_id=1, source_target_pairs={{0,2},{2,4},{4,6},{1,3},{3,5},{5,7},{8,10},{10,12},{12,14},{9,11},... | collective-permute-start | bytes 1544 | tf_op jit(solution)/shard_map/ppermute | solution.py:18
  100.4 5.8 %collective-permute-start.16 = (f32[42,1]{1,0:T(8,128)S(1)}, f32[42,1]{1,0:T(8,128)S(1)}, u32[]{:S(2)}, u32[]{:S(2)}) collective-permute-start(f32[42,1]{1,0:T(8,128)S(1)} %get-tuple-element.62), channel_id=1, source_target_pairs={{8,0},{16,8},{24,16},{9,1},{17,9},{25,17},{10,2},{18,10},{26,18},{... | collective-permute-start | bytes 512 | tf_op jit(solution)/shard_map/ppermute | solution.py:20
  102.3 6.6 %collective-permute-start.17 = (f32[42,1]{1,0:T(8,128)S(1)}, f32[42,1]{1,0:T(8,128)S(1)}, u32[]{:S(2)}, u32[]{:S(2)}) collective-permute-start(f32[42,1]{1,0:T(8,128)S(1)} %get-tuple-element.63), channel_id=1, source_target_pairs={{0,8},{8,16},{16,24},{1,9},{9,17},{17,25},{2,10},{10,18},{18,26},{... | collective-permute-start | bytes 512 | tf_op jit(solution)/shard_map/ppermute | solution.py:18
  109.8 3.8 %collective-permute-start.18 = (f32[1,128]{1,0:T(1,128)S(1)}, f32[1,128]{1,0:T(1,128)S(1)}, u32[]{:S(2)}, u32[]{:S(2)}) collective-permute-start(f32[1,128]{1,0:T(1,128)S(1)} %get-tuple-element.83), channel_id=1, source_target_pairs={{2,0},{4,2},{6,4},{3,1},{5,3},{7,5},{10,8},{12,10},{14,12},{11,9},... | collective-permute-start | bytes 1544 | tf_op jit(solution)/shard_map/ppermute | solution.py:20
  112.3 5.5 %collective-permute-start.19 = (f32[1,128]{1,0:T(1,128)S(1)}, f32[1,128]{1,0:T(1,128)S(1)}, u32[]{:S(2)}, u32[]{:S(2)}) collective-permute-start(f32[1,128]{1,0:T(1,128)S(1)} %get-tuple-element.82), channel_id=1, source_target_pairs={{0,2},{2,4},{4,6},{1,3},{3,5},{5,7},{8,10},{10,12},{12,14},{9,11},... | collective-permute-start | bytes 1544 | tf_op jit(solution)/shard_map/ppermute | solution.py:18
  117.8 5.8 %collective-permute-start.20 = (f32[42,1]{1,0:T(8,128)S(1)}, f32[42,1]{1,0:T(8,128)S(1)}, u32[]{:S(2)}, u32[]{:S(2)}) collective-permute-start(f32[42,1]{1,0:T(8,128)S(1)} %get-tuple-element.60), channel_id=1, source_target_pairs={{8,0},{16,8},{24,16},{9,1},{17,9},{25,17},{10,2},{18,10},{26,18},{... | collective-permute-start | bytes 512 | tf_op jit(solution)/shard_map/ppermute | solution.py:20
  119.7 6.6 %collective-permute-start.21 = (f32[42,1]{1,0:T(8,128)S(1)}, f32[42,1]{1,0:T(8,128)S(1)}, u32[]{:S(2)}, u32[]{:S(2)}) collective-permute-start(f32[42,1]{1,0:T(8,128)S(1)} %get-tuple-element.61), channel_id=1, source_target_pairs={{0,8},{8,16},{16,24},{1,9},{9,17},{17,25},{2,10},{10,18},{18,26},{... | collective-permute-start | bytes 512 | tf_op jit(solution)/shard_map/ppermute | solution.py:18
  127.3 3.2 %collective-permute-start.22 = (f32[1,128]{1,0:T(1,128)S(1)}, f32[1,128]{1,0:T(1,128)S(1)}, u32[]{:S(2)}, u32[]{:S(2)}) collective-permute-start(f32[1,128]{1,0:T(1,128)S(1)} %get-tuple-element.81), channel_id=1, source_target_pairs={{2,0},{4,2},{6,4},{3,1},{5,3},{7,5},{10,8},{12,10},{14,12},{11,9},... | collective-permute-start | bytes 1544 | tf_op jit(solution)/shard_map/ppermute | solution.py:20
  129.2 5.5 %collective-permute-start.23 = (f32[1,128]{1,0:T(1,128)S(1)}, f32[1,128]{1,0:T(1,128)S(1)}, u32[]{:S(2)}, u32[]{:S(2)}) collective-permute-start(f32[1,128]{1,0:T(1,128)S(1)} %get-tuple-element.80), channel_id=1, source_target_pairs={{0,2},{2,4},{4,6},{1,3},{3,5},{5,7},{8,10},{10,12},{12,14},{9,11},... | collective-permute-start | bytes 1544 | tf_op jit(solution)/shard_map/ppermute | solution.py:18
  134.8 5.8 %collective-permute-start.24 = (f32[42,1]{1,0:T(8,128)S(1)}, f32[42,1]{1,0:T(8,128)S(1)}, u32[]{:S(2)}, u32[]{:S(2)}) collective-permute-start(f32[42,1]{1,0:T(8,128)S(1)} %get-tuple-element.58), channel_id=1, source_target_pairs={{8,0},{16,8},{24,16},{9,1},{17,9},{25,17},{10,2},{18,10},{26,18},{... | collective-permute-start | bytes 512 | tf_op jit(solution)/shard_map/ppermute | solution.py:20
  136.7 6.6 %collective-permute-start.25 = (f32[42,1]{1,0:T(8,128)S(1)}, f32[42,1]{1,0:T(8,128)S(1)}, u32[]{:S(2)}, u32[]{:S(2)}) collective-permute-start(f32[42,1]{1,0:T(8,128)S(1)} %get-tuple-element.59), channel_id=1, source_target_pairs={{0,8},{8,16},{16,24},{1,9},{9,17},{17,25},{2,10},{10,18},{18,26},{... | collective-permute-start | bytes 512 | tf_op jit(solution)/shard_map/ppermute | solution.py:18
  144.2 3.2 %collective-permute-start.26 = (f32[1,128]{1,0:T(1,128)S(1)}, f32[1,128]{1,0:T(1,128)S(1)}, u32[]{:S(2)}, u32[]{:S(2)}) collective-permute-start(f32[1,128]{1,0:T(1,128)S(1)} %get-tuple-element.79), channel_id=1, source_target_pairs={{2,0},{4,2},{6,4},{3,1},{5,3},{7,5},{10,8},{12,10},{14,12},{11,9},... | collective-permute-start | bytes 1544 | tf_op jit(solution)/shard_map/ppermute | solution.py:20
  146.2 5.5 %collective-permute-start.27 = (f32[1,128]{1,0:T(1,128)S(1)}, f32[1,128]{1,0:T(1,128)S(1)}, u32[]{:S(2)}, u32[]{:S(2)}) collective-permute-start(f32[1,128]{1,0:T(1,128)S(1)} %get-tuple-element.78), channel_id=1, source_target_pairs={{0,2},{2,4},{4,6},{1,3},{3,5},{5,7},{8,10},{10,12},{12,14},{9,11},... | collective-permute-start | bytes 1544 | tf_op jit(solution)/shard_map/ppermute | solution.py:18
  151.7 5.8 %collective-permute-start.28 = (f32[42,1]{1,0:T(8,128)S(1)}, f32[42,1]{1,0:T(8,128)S(1)}, u32[]{:S(2)}, u32[]{:S(2)}) collective-permute-start(f32[42,1]{1,0:T(8,128)S(1)} %get-tuple-element.56), channel_id=1, source_target_pairs={{8,0},{16,8},{24,16},{9,1},{17,9},{25,17},{10,2},{18,10},{26,18},{... | collective-permute-start | bytes 512 | tf_op jit(solution)/shard_map/ppermute | solution.py:20
  153.6 6.6 %collective-permute-start.29 = (f32[42,1]{1,0:T(8,128)S(1)}, f32[42,1]{1,0:T(8,128)S(1)}, u32[]{:S(2)}, u32[]{:S(2)}) collective-permute-start(f32[42,1]{1,0:T(8,128)S(1)} %get-tuple-element.57), channel_id=1, source_target_pairs={{0,8},{8,16},{16,24},{1,9},{9,17},{17,25},{2,10},{10,18},{18,26},{... | collective-permute-start | bytes 512 | tf_op jit(solution)/shard_map/ppermute | solution.py:18
  160.4 3.2 %collective-permute-start.30 = (f32[1,128]{1,0:T(1,128)S(1)}, f32[1,128]{1,0:T(1,128)S(1)}, u32[]{:S(2)}, u32[]{:S(2)}) collective-permute-start(f32[1,128]{1,0:T(1,128)S(1)} %get-tuple-element.77), channel_id=1, source_target_pairs={{2,0},{4,2},{6,4},{3,1},{5,3},{7,5},{10,8},{12,10},{14,12},{11,9},... | collective-permute-start | bytes 1544 | tf_op jit(solution)/shard_map/ppermute | solution.py:20
  162.3 5.5 %collective-permute-start.31 = (f32[1,128]{1,0:T(1,128)S(1)}, f32[1,128]{1,0:T(1,128)S(1)}, u32[]{:S(2)}, u32[]{:S(2)}) collective-permute-start(f32[1,128]{1,0:T(1,128)S(1)} %get-tuple-element.76), channel_id=1, source_target_pairs={{0,2},{2,4},{4,6},{1,3},{3,5},{5,7},{8,10},{10,12},{12,14},{9,11},... | collective-permute-start | bytes 1544 | tf_op jit(solution)/shard_map/ppermute | solution.py:18
  167.8 5.8 %collective-permute-start.32 = (f32[42,1]{1,0:T(8,128)S(1)}, f32[42,1]{1,0:T(8,128)S(1)}, u32[]{:S(2)}, u32[]{:S(2)}) collective-permute-start(f32[42,1]{1,0:T(8,128)S(1)} %get-tuple-element.54), channel_id=1, source_target_pairs={{8,0},{16,8},{24,16},{9,1},{17,9},{25,17},{10,2},{18,10},{26,18},{... | collective-permute-start | bytes 512 | tf_op jit(solution)/shard_map/ppermute | solution.py:20
  169.7 6.7 %collective-permute-start.33 = (f32[42,1]{1,0:T(8,128)S(1)}, f32[42,1]{1,0:T(8,128)S(1)}, u32[]{:S(2)}, u32[]{:S(2)}) collective-permute-start(f32[42,1]{1,0:T(8,128)S(1)} %get-tuple-element.55), channel_id=1, source_target_pairs={{0,8},{8,16},{16,24},{1,9},{9,17},{17,25},{2,10},{10,18},{18,26},{... | collective-permute-start | bytes 512 | tf_op jit(solution)/shard_map/ppermute | solution.py:18
  176.5 3.4 %collective-permute-start.34 = (f32[1,128]{1,0:T(1,128)S(1)}, f32[1,128]{1,0:T(1,128)S(1)}, u32[]{:S(2)}, u32[]{:S(2)}) collective-permute-start(f32[1,128]{1,0:T(1,128)S(1)} %get-tuple-element.75), channel_id=1, source_target_pairs={{2,0},{4,2},{6,4},{3,1},{5,3},{7,5},{10,8},{12,10},{14,12},{11,9},... | collective-permute-start | bytes 1544 | tf_op jit(solution)/shard_map/ppermute | solution.py:20
  178.6 5.5 %collective-permute-start.35 = (f32[1,128]{1,0:T(1,128)S(1)}, f32[1,128]{1,0:T(1,128)S(1)}, u32[]{:S(2)}, u32[]{:S(2)}) collective-permute-start(f32[1,128]{1,0:T(1,128)S(1)} %get-tuple-element.74), channel_id=1, source_target_pairs={{0,2},{2,4},{4,6},{1,3},{3,5},{5,7},{8,10},{10,12},{12,14},{9,11},... | collective-permute-start | bytes 1544 | tf_op jit(solution)/shard_map/ppermute | solution.py:18
  184.1 5.8 %collective-permute-start.36 = (f32[42,1]{1,0:T(8,128)S(1)}, f32[42,1]{1,0:T(8,128)S(1)}, u32[]{:S(2)}, u32[]{:S(2)}) collective-permute-start(f32[42,1]{1,0:T(8,128)S(1)} %get-tuple-element.52), channel_id=1, source_target_pairs={{8,0},{16,8},{24,16},{9,1},{17,9},{25,17},{10,2},{18,10},{26,18},{... | collective-permute-start | bytes 512 | tf_op jit(solution)/shard_map/ppermute | solution.py:20
  186.1 6.6 %collective-permute-start.37 = (f32[42,1]{1,0:T(8,128)S(1)}, f32[42,1]{1,0:T(8,128)S(1)}, u32[]{:S(2)}, u32[]{:S(2)}) collective-permute-start(f32[42,1]{1,0:T(8,128)S(1)} %get-tuple-element.53), channel_id=1, source_target_pairs={{0,8},{8,16},{16,24},{1,9},{9,17},{17,25},{2,10},{10,18},{18,26},{... | collective-permute-start | bytes 512 | tf_op jit(solution)/shard_map/ppermute | solution.py:18
  192.8 16.6 %copy-start.16 = (f32[40,128]{1,0:T(8,128)}, f32[40,128]{1,0:T(8,128)S(1)}, u32[]{:S(2)}) copy-start(f32[40,128]{1,0:T(8,128)S(1)} %fusion.73) | copy-start | bytes 61444
  192.8 3.2 %collective-permute-start.38 = (f32[1,128]{1,0:T(1,128)S(1)}, f32[1,128]{1,0:T(1,128)S(1)}, u32[]{:S(2)}, u32[]{:S(2)}) collective-permute-start(f32[1,128]{1,0:T(1,128)S(1)} %get-tuple-element.73), channel_id=1, source_target_pairs={{2,0},{4,2},{6,4},{3,1},{5,3},{7,5},{10,8},{12,10},{14,12},{11,9},... | collective-permute-start | bytes 1544 | tf_op jit(solution)/shard_map/ppermute | solution.py:20
  194.7 5.5 %collective-permute-start.39 = (f32[1,128]{1,0:T(1,128)S(1)}, f32[1,128]{1,0:T(1,128)S(1)}, u32[]{:S(2)}, u32[]{:S(2)}) collective-permute-start(f32[1,128]{1,0:T(1,128)S(1)} %get-tuple-element.72), channel_id=1, source_target_pairs={{0,2},{2,4},{4,6},{1,3},{3,5},{5,7},{8,10},{10,12},{12,14},{9,11},... | collective-permute-start | bytes 1544 | tf_op jit(solution)/shard_map/ppermute | solution.py:18
  200.3 6.1 %collective-permute-start.40 = (f32[42,1]{1,0:T(8,128)S(1)}, f32[42,1]{1,0:T(8,128)S(1)}, u32[]{:S(2)}, u32[]{:S(2)}) collective-permute-start(f32[42,1]{1,0:T(8,128)S(1)} %get-tuple-element.50), channel_id=1, source_target_pairs={{8,0},{16,8},{24,16},{9,1},{17,9},{25,17},{10,2},{18,10},{26,18},{... | collective-permute-start | bytes 512 | tf_op jit(solution)/shard_map/ppermute | solution.py:20
  202.2 6.6 %collective-permute-start.41 = (f32[42,1]{1,0:T(8,128)S(1)}, f32[42,1]{1,0:T(8,128)S(1)}, u32[]{:S(2)}, u32[]{:S(2)}) collective-permute-start(f32[42,1]{1,0:T(8,128)S(1)} %get-tuple-element.51), channel_id=1, source_target_pairs={{0,8},{8,16},{16,24},{1,9},{9,17},{17,25},{2,10},{10,18},{18,26},{... | collective-permute-start | bytes 512 | tf_op jit(solution)/shard_map/ppermute | solution.py:18
  (29 other events, 40.5 us)
Sparse Core Ops, SparseCore 0:
  51.8 20.4 all-reduce.3
where the time goes:
time: 223 us; the launch traced here: 221 us
  starting transfers between devices  100 us (45%)
  waiting for transfers between devices  73.7 us (33%)
  other arithmetic  16.3 us (7%)
  between operations  15.4 us (7%)
  local copies, waits for them, and re-layouts  15.1 us (7%)
    ppermute x21, waiting for transfers between devices, extended(): lax.ppermute(tail, axis, [(i, (i + 1) % count) for i in range(ends)])  60.6 us
    ppermute x21, starting transfers between devices, extended(): lax.ppermute(head, axis, [((i + 1) % count, i) for i in range(ends)])  50 us
    ppermute x21, starting transfers between devices, extended(): lax.ppermute(tail, axis, [(i, (i + 1) % count) for i in range(ends)])  49.9 us
    psum x1, waiting for transfers between devices, per_device(): totals = lax.psum(planes, 'gz')  9.72 us
    unnamed x116, local copies, waits for them, and re-layouts  5.28 us
  transfers between devices with their start and end apart: 43, of which 21 were waited for; matrix products, arithmetic and copies ran while one was open for 4% of the time, Pallas kernels for 0%

commit v1 on v0

--- a/solution.py
+++ b/solution.py
@@ -146,7 +146,7 @@
         padded[:3], weights, storage, storage_rows, coupling_rows
     )
     planes = coarse_planes(residual, weights, storage, storage_rows, coupling_rows)
-    totals = lax.psum(planes, "gz")
+    totals = lax.all_gather(planes, "gz").sum(axis=0)
     correction = jnp.zeros(totals.shape[1:], jnp.float32)
     for repeat_index in range(SWEEPS):
         bordered = extended(correction, (("gy", 0), ("gx", 1)), 1)

time: 223 us -> 198 us (0.89)
  waiting for transfers between devices: 73.7 us -> 57 us
  between operations: 15.4 us -> 2.1 us
  starting transfers between devices: 100 us -> 104 us
  other arithmetic: 16.3 us -> 12.9 us
  local copies, waits for them, and re-layouts: 15.1 us -> 18.5 us
    psum x1 -> x0, waiting for transfers between devices: 9.72 us -> none  [per_device(): totals = lax.psum(planes, 'gz')]
    ppermute x21, waiting for transfers between devices: 60.6 us -> 55.3 us  [extended(): lax.ppermute(tail, axis, [(i, (i + 1) % count) for i in range(ends)])]
    add x7, other arithmetic: 3.91 us -> 0.65 us  [jacobi(): return field + relax * (planes[0] - diagonal * field + nearby) / diagonal]
    ppermute x21, starting transfers between devices: 49.9 us -> 52.6 us  [extended(): lax.ppermute(tail, axis, [(i, (i + 1) % count) for i in range(ends)])]
    unnamed x116 -> x126, local copies, waits for them, and re-layouts: 5.28 us -> 7.41 us
  transfers between devices with their start and end apart: 43 -> 42, of which waited for: 21 -> 17; matrix products, arithmetic and copies ran while one was open for 4% -> 9% of each run, Pallas kernels for 0% -> 0%
where the time goes in v1:
time: 198 us; the launch traced here: 197 us
  starting transfers between devices  104 us (53%)
  waiting for transfers between devices  57 us (29%)
  local copies, waits for them, and re-layouts  18.5 us (9%)
  other arithmetic  12.9 us (7%)
  blocking collectives  2.18 us (1%)
  between operations  2.1 us (1%)
    ppermute x21, waiting for transfers between devices, extended(): lax.ppermute(tail, axis, [(i, (i + 1) % count) for i in range(ends)])  55.3 us
    ppermute x21, starting transfers between devices, extended(): lax.ppermute(tail, axis, [(i, (i + 1) % count) for i in range(ends)])  52.6 us
    ppermute x21, starting transfers between devices, extended(): lax.ppermute(head, axis, [((i + 1) % count, i) for i in range(ends)])  51.2 us
    unnamed x126, local copies, waits for them, and re-layouts  7.41 us
  transfers between devices with their start and end apart: 42, of which 17 were waited for; matrix products, arithmetic and copies ran while one was open for 9% of the time, Pallas kernels for 0%

profile of v1, /device:TPU:28, one launch (start us, length us, event | category | flops | bytes accessed | tf_op | source)
XLA Modules:
  0.0 196.8 jit_solution(7702420557982893749)
XLA Ops:
  1.9 2.3 %collective-permute-start.6 = (f32[1,128]{1,0:T(1,128)S(1)}, f32[1,128]{1,0:T(1,128)S(1)}, u32[]{:S(2)}, u32[]{:S(2)}) collective-permute-start(f32[1,128]{1,0:T(1,128)S(1)} %broadcast.60), channel_id=1, source_target_pairs={{2,0},{4,2},{6,4},{3,1},{5,3},{7,5},{10,8},{12,10},{14,12},{11,9},... | collective-permute-start | bytes 1544 | tf_op jit(solution)/shard_map/ppermute | solution.py:20
  4.3 1.3 collective-permute-start.7
  5.7 1.5 collective-permute-start
  7.1 1.3 collective-permute-start.1
  10.4 1.3 collective-permute-start.2
  11.7 5.0 %collective-permute-start.3 = (f32[4,18,1,128]{3,0,2,1:T(4,128)S(1)}, f32[4,18,1,128]{3,0,2,1:T(4,128)S(1)}, u32[]{:S(2)}, u32[]{:S(2)}) collective-permute-start(f32[4,18,1,128]{3,0,2,1:T(4,128)S(1)} %copy.239), channel_id=1, source_target_pairs={{2,0},{4,2},{6,4},{3,1},{5,3},{7,5},{10,8},{12,10},{14,12},{11,9},... | collective-permute-start | bytes 110600 | tf_op jit(solution)/shard_map/ppermute | solution.py:20
  16.8 1.6 collective-permute-done.3
  18.7 1.8 fusion.155
  20.5 2.2 %copy.212 = f32[4,18,42,1]{2,0,3,1:T(4,128)S(1)} copy(f32[4,18,42,1]{3,2,1,0:T(8,128)} %get-tuple-element.29) | data formatting | bytes 24192 | tf_op jit(solution)/shard_map/slice | solution.py:15
  22.6 3.4 %collective-permute-start.4 = (f32[4,18,42,1]{2,0,3,1:T(4,128)S(1)}, f32[4,18,42,1]{2,0,3,1:T(4,128)S(1)}, u32[]{:S(2)}, u32[]{:S(2)}) collective-permute-start(f32[4,18,42,1]{2,0,3,1:T(4,128)S(1)} %copy.212), channel_id=1, source_target_pairs={{0,8},{8,16},{16,24},{1,9},{9,17},{17,25},{2,10},{10,18},{18,26},{... | collective-permute-start | bytes 36296 | tf_op jit(solution)/shard_map/ppermute | solution.py:18
  26.8 3.3 %collective-permute-start.5 = (f32[4,18,42,1]{2,0,3,1:T(4,128)S(1)}, f32[4,18,42,1]{2,0,3,1:T(4,128)S(1)}, u32[]{:S(2)}, u32[]{:S(2)}) collective-permute-start(f32[4,18,42,1]{2,0,3,1:T(4,128)S(1)} %copy.213), channel_id=1, source_target_pairs={{8,0},{16,8},{24,16},{9,1},{17,9},{25,17},{10,2},{18,10},{26,18},{... | collective-permute-start | bytes 36296 | tf_op jit(solution)/shard_map/ppermute | solution.py:20
  30.8 2.4 %collective-permute-start.8 = (f32[42,1]{1,0:T(8,128)}, f32[42,1]{1,0:T(8,128)}, u32[]{:S(2)}, u32[]{:S(2)}) collective-permute-start(f32[42,1]{1,0:T(8,128)} %get-tuple-element.64), channel_id=1, source_target_pairs={{8,0},{16,8},{24,16},{9,1},{17,9},{25,17},{10,2},{18,10},{26,18},{... | collective-permute-start | bytes 512 | tf_op jit(solution)/shard_map/ppermute | solution.py:20
  33.2 4.0 %collective-permute-start.9 = (f32[42,1]{1,0:T(8,128)}, f32[42,1]{1,0:T(8,128)}, u32[]{:S(2)}, u32[]{:S(2)}) collective-permute-start(f32[42,1]{1,0:T(8,128)} %get-tuple-element.65), channel_id=1, source_target_pairs={{0,8},{8,16},{16,24},{1,9},{9,17},{17,25},{2,10},{10,18},{18,26},{... | collective-permute-start | bytes 512 | tf_op jit(solution)/shard_map/ppermute | solution.py:18
  38.0 1.9 copy.215
  39.9 1.5 fusion.24
  42.9 3.3 %fusion.2 = f32[3,16,40,128]{3,2,1,0:T(8,128)S(1)} fusion(f32[3,16,40,128]{3,2,1,0:T(8,128)S(1)} %copy.247, f32[4,18,42,1]{3,2,1,0:T(8,128)S(1)} %copy.214, f32[4,18,1,128]{3,2,1,0:T(1,128)S(1)} %copy.211, f32[4,18,1,128]{3,2,1,0:T(1,128)S(1)} %copy.210, f32[4,1,40,128]{3,2,1,0:T(8,128)S(1)} %collective-permute-done.1, ...), kind=kLoop, calls=%fused_computation.18 | loop fusion | flops 10076160 | bytes 4521600 | tf_op jit(solution)/shard_map/add | solution.py:56
  53.3 2.2 %all-gather = f32[12,40,128]{2,1,0:T(8,128)S(1)} all-gather(f32[6,40,128]{2,1,0:T(8,128)} %constant_dynamic-update-slice_fusion), channel_id=2, replica_groups=mesh['gx'=4,'gy'=4,'gz'=2] {'gz'}, dimensions={0}, use_global_device_ids=true | all-gather | bytes 368640 | tf_op jit(solution)/shard_map/all_gather | solution.py:149
  56.4 4.4 %collective-permute-start.10 = (f32[1,128]{1,0:T(1,128)S(1)}, f32[1,128]{1,0:T(1,128)S(1)}, u32[]{:S(2)}, u32[]{:S(2)}) collective-permute-start(f32[1,128]{1,0:T(1,128)S(1)} %get-tuple-element.85), channel_id=1, source_target_pairs={{2,0},{4,2},{6,4},{3,1},{5,3},{7,5},{10,8},{12,10},{14,12},{11,9},... | collective-permute-start | bytes 1544 | tf_op jit(solution)/shard_map/ppermute | solution.py:20
  60.8 1.4 collective-permute-start.11
  62.3 4.2 %collective-permute-done.11 = f32[1,128]{1,0:T(1,128)S(1)} collective-permute-done((f32[1,128]{1,0:T(1,128)S(1)}, f32[1,128]{1,0:T(1,128)S(1)}, u32[]{:S(2)}, u32[]{:S(2)}) %collective-permute-start.11) | collective-permute-done | bytes 544 | tf_op jit(solution)/shard_map/ppermute | solution.py:18
  66.5 2.7 %collective-permute-start.12 = (f32[42,1]{1,0:T(8,128)S(1)}, f32[42,1]{1,0:T(8,128)S(1)}, u32[]{:S(2)}, u32[]{:S(2)}) collective-permute-start(f32[42,1]{1,0:T(8,128)S(1)} %get-tuple-element.62), channel_id=1, source_target_pairs={{8,0},{16,8},{24,16},{9,1},{17,9},{25,17},{10,2},{18,10},{26,18},{... | collective-permute-start | bytes 512 | tf_op jit(solution)/shard_map/ppermute | solution.py:20
  69.3 3.1 %collective-permute-start.13 = (f32[42,1]{1,0:T(8,128)S(1)}, f32[42,1]{1,0:T(8,128)S(1)}, u32[]{:S(2)}, u32[]{:S(2)}) collective-permute-start(f32[42,1]{1,0:T(8,128)S(1)} %get-tuple-element.63), channel_id=1, source_target_pairs={{0,8},{8,16},{16,24},{1,9},{9,17},{17,25},{2,10},{10,18},{18,26},{... | collective-permute-start | bytes 512 | tf_op jit(solution)/shard_map/ppermute | solution.py:18
  72.4 3.5 %collective-permute-done.13 = f32[42,1]{1,0:T(8,128)S(1)} collective-permute-done((f32[42,1]{1,0:T(8,128)S(1)}, f32[42,1]{1,0:T(8,128)S(1)}, u32[]{:S(2)}, u32[]{:S(2)}) %collective-permute-start.13) | collective-permute-done | bytes 200 | tf_op jit(solution)/shard_map/ppermute | solution.py:18
  76.0 3.9 %collective-permute-start.14 = (f32[1,128]{1,0:T(1,128)S(1)}, f32[1,128]{1,0:T(1,128)S(1)}, u32[]{:S(2)}, u32[]{:S(2)}) collective-permute-start(f32[1,128]{1,0:T(1,128)S(1)} %get-tuple-element.83), channel_id=1, source_target_pairs={{2,0},{4,2},{6,4},{3,1},{5,3},{7,5},{10,8},{12,10},{14,12},{11,9},... | collective-permute-start | bytes 1544 | tf_op jit(solution)/shard_map/ppermute | solution.py:20
  79.9 1.3 collective-permute-start.15
  81.2 4.2 %collective-permute-done.15 = f32[1,128]{1,0:T(1,128)S(1)} collective-permute-done((f32[1,128]{1,0:T(1,128)S(1)}, f32[1,128]{1,0:T(1,128)S(1)}, u32[]{:S(2)}, u32[]{:S(2)}) %collective-permute-start.15) | collective-permute-done | bytes 544 | tf_op jit(solution)/shard_map/ppermute | solution.py:18
  85.5 1.9 collective-permute-start.16
  87.4 3.9 %collective-permute-start.17 = (f32[42,1]{1,0:T(8,128)S(1)}, f32[42,1]{1,0:T(8,128)S(1)}, u32[]{:S(2)}, u32[]{:S(2)}) collective-permute-start(f32[42,1]{1,0:T(8,128)S(1)} %get-tuple-element.61), channel_id=1, source_target_pairs={{0,8},{8,16},{16,24},{1,9},{9,17},{17,25},{2,10},{10,18},{18,26},{... | collective-permute-start | bytes 512 | tf_op jit(solution)/shard_map/ppermute | solution.py:18
  91.3 2.7 %collective-permute-done.17 = f32[42,1]{1,0:T(8,128)S(1)} collective-permute-done((f32[42,1]{1,0:T(8,128)S(1)}, f32[42,1]{1,0:T(8,128)S(1)}, u32[]{:S(2)}, u32[]{:S(2)}) %collective-permute-start.17) | collective-permute-done | bytes 200 | tf_op jit(solution)/shard_map/ppermute | solution.py:18
  94.1 2.4 %collective-permute-start.18 = (f32[1,128]{1,0:T(1,128)S(1)}, f32[1,128]{1,0:T(1,128)S(1)}, u32[]{:S(2)}, u32[]{:S(2)}) collective-permute-start(f32[1,128]{1,0:T(1,128)S(1)} %get-tuple-element.81), channel_id=1, source_target_pairs={{2,0},{4,2},{6,4},{3,1},{5,3},{7,5},{10,8},{12,10},{14,12},{11,9},... | collective-permute-start | bytes 1544 | tf_op jit(solution)/shard_map/ppermute | solution.py:20
  96.5 1.3 collective-permute-start.19
  97.8 4.2 %collective-permute-done.19 = f32[1,128]{1,0:T(1,128)S(1)} collective-permute-done((f32[1,128]{1,0:T(1,128)S(1)}, f32[1,128]{1,0:T(1,128)S(1)}, u32[]{:S(2)}, u32[]{:S(2)}) %collective-permute-start.19) | collective-permute-done | bytes 544 | tf_op jit(solution)/shard_map/ppermute | solution.py:18
  102.0 1.9 collective-permute-start.20
  104.0 3.9 %collective-permute-start.21 = (f32[42,1]{1,0:T(8,128)S(1)}, f32[42,1]{1,0:T(8,128)S(1)}, u32[]{:S(2)}, u32[]{:S(2)}) collective-permute-start(f32[42,1]{1,0:T(8,128)S(1)} %get-tuple-element.59), channel_id=1, source_target_pairs={{0,8},{8,16},{16,24},{1,9},{9,17},{17,25},{2,10},{10,18},{18,26},{... | collective-permute-start | bytes 512 | tf_op jit(solution)/shard_map/ppermute | solution.py:18
  107.9 2.7 %collective-permute-done.21 = f32[42,1]{1,0:T(8,128)S(1)} collective-permute-done((f32[42,1]{1,0:T(8,128)S(1)}, f32[42,1]{1,0:T(8,128)S(1)}, u32[]{:S(2)}, u32[]{:S(2)}) %collective-permute-start.21) | collective-permute-done | bytes 200 | tf_op jit(solution)/shard_map/ppermute | solution.py:18
  110.7 1.9 collective-permute-start.22
  112.6 1.3 collective-permute-start.23
  113.9 4.2 %collective-permute-done.23 = f32[1,128]{1,0:T(1,128)S(1)} collective-permute-done((f32[1,128]{1,0:T(1,128)S(1)}, f32[1,128]{1,0:T(1,128)S(1)}, u32[]{:S(2)}, u32[]{:S(2)}) %collective-permute-start.23) | collective-permute-done | bytes 544 | tf_op jit(solution)/shard_map/ppermute | solution.py:18
  118.2 1.9 collective-permute-start.24
  120.1 3.9 %collective-permute-start.25 = (f32[42,1]{1,0:T(8,128)S(1)}, f32[42,1]{1,0:T(8,128)S(1)}, u32[]{:S(2)}, u32[]{:S(2)}) collective-permute-start(f32[42,1]{1,0:T(8,128)S(1)} %get-tuple-element.57), channel_id=1, source_target_pairs={{0,8},{8,16},{16,24},{1,9},{9,17},{17,25},{2,10},{10,18},{18,26},{... | collective-permute-start | bytes 512 | tf_op jit(solution)/shard_map/ppermute | solution.py:18
  124.0 2.7 %collective-permute-done.25 = f32[42,1]{1,0:T(8,128)S(1)} collective-permute-done((f32[42,1]{1,0:T(8,128)S(1)}, f32[42,1]{1,0:T(8,128)S(1)}, u32[]{:S(2)}, u32[]{:S(2)}) %collective-permute-start.25) | collective-permute-done | bytes 200 | tf_op jit(solution)/shard_map/ppermute | solution.py:18
  126.8 2.0 %collective-permute-start.26 = (f32[1,128]{1,0:T(1,128)S(1)}, f32[1,128]{1,0:T(1,128)S(1)}, u32[]{:S(2)}, u32[]{:S(2)}) collective-permute-start(f32[1,128]{1,0:T(1,128)S(1)} %get-tuple-element.77), channel_id=1, source_target_pairs={{2,0},{4,2},{6,4},{3,1},{5,3},{7,5},{10,8},{12,10},{14,12},{11,9},... | collective-permute-start | bytes 1544 | tf_op jit(solution)/shard_map/ppermute | solution.py:20
  128.8 1.3 collective-permute-start.27
  130.2 4.2 %collective-permute-done.27 = f32[1,128]{1,0:T(1,128)S(1)} collective-permute-done((f32[1,128]{1,0:T(1,128)S(1)}, f32[1,128]{1,0:T(1,128)S(1)}, u32[]{:S(2)}, u32[]{:S(2)}) %collective-permute-start.27) | collective-permute-done | bytes 544 | tf_op jit(solution)/shard_map/ppermute | solution.py:18
  134.4 1.9 collective-permute-start.28
  136.3 3.9 %collective-permute-start.29 = (f32[42,1]{1,0:T(8,128)S(1)}, f32[42,1]{1,0:T(8,128)S(1)}, u32[]{:S(2)}, u32[]{:S(2)}) collective-permute-start(f32[42,1]{1,0:T(8,128)S(1)} %get-tuple-element.55), channel_id=1, source_target_pairs={{0,8},{8,16},{16,24},{1,9},{9,17},{17,25},{2,10},{10,18},{18,26},{... | collective-permute-start | bytes 512 | tf_op jit(solution)/shard_map/ppermute | solution.py:18
  140.2 2.7 %collective-permute-done.29 = f32[42,1]{1,0:T(8,128)S(1)} collective-permute-done((f32[42,1]{1,0:T(8,128)S(1)}, f32[42,1]{1,0:T(8,128)S(1)}, u32[]{:S(2)}, u32[]{:S(2)}) %collective-permute-start.29) | collective-permute-done | bytes 200 | tf_op jit(solution)/shard_map/ppermute | solution.py:18
  143.0 2.0 collective-permute-start.30
  145.0 1.3 collective-permute-start.31
  146.3 4.2 %collective-permute-done.31 = f32[1,128]{1,0:T(1,128)S(1)} collective-permute-done((f32[1,128]{1,0:T(1,128)S(1)}, f32[1,128]{1,0:T(1,128)S(1)}, u32[]{:S(2)}, u32[]{:S(2)}) %collective-permute-start.31) | collective-permute-done | bytes 544 | tf_op jit(solution)/shard_map/ppermute | solution.py:18
  150.5 1.9 collective-permute-start.32
  152.5 3.9 %collective-permute-start.33 = (f32[42,1]{1,0:T(8,128)S(1)}, f32[42,1]{1,0:T(8,128)S(1)}, u32[]{:S(2)}, u32[]{:S(2)}) collective-permute-start(f32[42,1]{1,0:T(8,128)S(1)} %get-tuple-element.53), channel_id=1, source_target_pairs={{0,8},{8,16},{16,24},{1,9},{9,17},{17,25},{2,10},{10,18},{18,26},{... | collective-permute-start | bytes 512 | tf_op jit(solution)/shard_map/ppermute | solution.py:18
  156.4 2.7 %collective-permute-done.33 = f32[42,1]{1,0:T(8,128)S(1)} collective-permute-done((f32[42,1]{1,0:T(8,128)S(1)}, f32[42,1]{1,0:T(8,128)S(1)}, u32[]{:S(2)}, u32[]{:S(2)}) %collective-permute-start.33) | collective-permute-done | bytes 200 | tf_op jit(solution)/shard_map/ppermute | solution.py:18
  159.2 1.9 collective-permute-start.34
  162.4 4.2 %collective-permute-done.35 = f32[1,128]{1,0:T(1,128)S(1)} collective-permute-done((f32[1,128]{1,0:T(1,128)S(1)}, f32[1,128]{1,0:T(1,128)S(1)}, u32[]{:S(2)}, u32[]{:S(2)}) %collective-permute-start.35) | collective-permute-done | bytes 544 | tf_op jit(solution)/shard_map/ppermute | solution.py:18
  166.7 1.9 collective-permute-start.36
  168.6 3.9 %collective-permute-start.37 = (f32[42,1]{1,0:T(8,128)S(1)}, f32[42,1]{1,0:T(8,128)S(1)}, u32[]{:S(2)}, u32[]{:S(2)}) collective-permute-start(f32[42,1]{1,0:T(8,128)S(1)} %get-tuple-element.51), channel_id=1, source_target_pairs={{0,8},{8,16},{16,24},{1,9},{9,17},{17,25},{2,10},{10,18},{18,26},{... | collective-permute-start | bytes 512 | tf_op jit(solution)/shard_map/ppermute | solution.py:18
  172.6 2.7 %collective-permute-done.37 = f32[42,1]{1,0:T(8,128)S(1)} collective-permute-done((f32[42,1]{1,0:T(8,128)S(1)}, f32[42,1]{1,0:T(8,128)S(1)}, u32[]{:S(2)}, u32[]{:S(2)}) %collective-permute-start.37) | collective-permute-done | bytes 200 | tf_op jit(solution)/shard_map/ppermute | solution.py:18
  175.4 2.2 %collective-permute-start.38 = (f32[1,128]{1,0:T(1,128)S(1)}, f32[1,128]{1,0:T(1,128)S(1)}, u32[]{:S(2)}, u32[]{:S(2)}) collective-permute-start(f32[1,128]{1,0:T(1,128)S(1)} %get-tuple-element.71), channel_id=1, source_target_pairs={{2,0},{4,2},{6,4},{3,1},{5,3},{7,5},{10,8},{12,10},{14,12},{11,9},... | collective-permute-start | bytes 1544 | tf_op jit(solution)/shard_map/ppermute | solution.py:20
  177.5 1.3 collective-permute-start.39
  178.9 4.2 %collective-permute-done.39 = f32[1,128]{1,0:T(1,128)S(1)} collective-permute-done((f32[1,128]{1,0:T(1,128)S(1)}, f32[1,128]{1,0:T(1,128)S(1)}, u32[]{:S(2)}, u32[]{:S(2)}) %collective-permute-start.39) | collective-permute-done | bytes 544 | tf_op jit(solution)/shard_map/ppermute | solution.py:18
  183.1 1.9 collective-permute-start.40
  185.0 4.1 %collective-permute-start.41 = (f32[42,1]{1,0:T(8,128)S(1)}, f32[42,1]{1,0:T(8,128)S(1)}, u32[]{:S(2)}, u32[]{:S(2)}) collective-permute-start(f32[42,1]{1,0:T(8,128)S(1)} %get-tuple-element.49), channel_id=1, source_target_pairs={{0,8},{8,16},{16,24},{1,9},{9,17},{17,25},{2,10},{10,18},{18,26},{... | collective-permute-start | bytes 512 | tf_op jit(solution)/shard_map/ppermute | solution.py:18
  189.2 2.5 %collective-permute-done.41 = f32[42,1]{1,0:T(8,128)S(1)} collective-permute-done((f32[42,1]{1,0:T(8,128)S(1)}, f32[42,1]{1,0:T(8,128)S(1)}, u32[]{:S(2)}, u32[]{:S(2)}) %collective-permute-start.41) | collective-permute-done | bytes 200 | tf_op jit(solution)/shard_map/ppermute | solution.py:18
  (225 shorter events, 22.5 us)
Async XLA Ops:
  0.6 5.0 %copy-start.16 = (bf16[16,40,128]{2,1,0:T(8,128)(2,1)S(1)}, bf16[16,40,128]{2,1,0:T(8,128)(2,1)}, u32[]{:S(2)}) copy-start(bf16[16,40,128]{2,1,0:T(8,128)(2,1)} %param.11) | copy-start | bytes 491524
  0.6 7.9 %copy-start.54 = (s32[16]{0:T(128)S(1)}, s32[16]{0:T(128)}, u32[]{:S(2)}) copy-start(s32[16]{0:T(128)} %param.13) | copy-start | bytes 196
  0.7 8.7 %copy-start.51 = (f32[4,3,3]{2,0,1:T(4,128)S(1)}, f32[4,3,3]{2,0,1:T(4,128)}, u32[]{:S(2)}) copy-start(f32[4,3,3]{2,0,1:T(4,128)} %param.14) | copy-start | bytes 436
  0.7 7.8 %copy-start.50 = (f32[4,3,3]{2,0,1:T(4,128)S(1)}, f32[4,3,3]{2,0,1:T(4,128)}, u32[]{:S(2)}) copy-start(f32[4,3,3]{2,0,1:T(4,128)} %param.15) | copy-start | bytes 436
  1.9 14.8 %collective-permute-start.6 = (f32[1,128]{1,0:T(1,128)S(1)}, f32[1,128]{1,0:T(1,128)S(1)}, u32[]{:S(2)}, u32[]{:S(2)}) collective-permute-start(f32[1,128]{1,0:T(1,128)S(1)} %broadcast.60), channel_id=1, source_target_pairs={{2,0},{4,2},{6,4},{3,1},{5,3},{7,5},{10,8},{12,10},{14,12},{11,9},... | collective-permute-start | bytes 1544 | tf_op jit(solution)/shard_map/ppermute | solution.py:20
  4.3 12.4 %collective-permute-start.7 = (f32[1,128]{1,0:T(1,128)S(1)}, f32[1,128]{1,0:T(1,128)S(1)}, u32[]{:S(2)}, u32[]{:S(2)}) collective-permute-start(f32[1,128]{1,0:T(1,128)S(1)} %broadcast.60), channel_id=1, source_target_pairs={{0,2},{2,4},{4,6},{1,3},{3,5},{5,7},{8,10},{10,12},{12,14},{9,11},... | collective-permute-start | bytes 1544 | tf_op jit(solution)/shard_map/ppermute | solution.py:18
  5.7 4.6 %collective-permute-start = (f32[4,1,40,128]{3,2,1,0:T(8,128)S(1)}, f32[4,1,40,128]{3,2,1,0:T(8,128)S(1)}, u32[]{:S(2)}, u32[]{:S(2)}) collective-permute-start(f32[4,1,40,128]{3,2,1,0:T(8,128)S(1)} %get-tuple-element.32), channel_id=1, source_target_pairs={{0,1},{2,3},{4,5},{6,7},{8,9},{10,11},{12,13},{14,15},{16,17},{18,... | collective-permute-start | bytes 245768 | tf_op jit(solution)/shard_map/ppermute | solution.py:18
  7.1 3.2 %collective-permute-start.1 = (f32[4,1,40,128]{3,2,1,0:T(8,128)S(1)}, f32[4,1,40,128]{3,2,1,0:T(8,128)S(1)}, u32[]{:S(2)}, u32[]{:S(2)}) collective-permute-start(f32[4,1,40,128]{3,2,1,0:T(8,128)S(1)} %get-tuple-element.33), channel_id=1, source_target_pairs={{1,0},{3,2},{5,4},{7,6},{9,8},{11,10},{13,12},{15,14},{17,16},{19,... | collective-permute-start | bytes 245768 | tf_op jit(solution)/shard_map/ppermute | solution.py:20
  9.4 37.3 %copy-start.19 = (f32[16]{0:T(128)}, f32[16]{0:T(128)S(1)}, u32[]{:S(2)}) copy-start(f32[16]{0:T(128)S(1)} %get-tuple-element.101) | copy-start | bytes 196
  10.4 6.4 %collective-permute-start.2 = (f32[4,18,1,128]{3,0,2,1:T(4,128)S(1)}, f32[4,18,1,128]{3,0,2,1:T(4,128)S(1)}, u32[]{:S(2)}, u32[]{:S(2)}) collective-permute-start(f32[4,18,1,128]{3,0,2,1:T(4,128)S(1)} %copy.238), channel_id=1, source_target_pairs={{0,2},{2,4},{4,6},{1,3},{3,5},{5,7},{8,10},{10,12},{12,14},{9,11},... | collective-permute-start | bytes 110600 | tf_op jit(solution)/shard_map/ppermute | solution.py:18
  11.7 6.7 %collective-permute-start.3 = (f32[4,18,1,128]{3,0,2,1:T(4,128)S(1)}, f32[4,18,1,128]{3,0,2,1:T(4,128)S(1)}, u32[]{:S(2)}, u32[]{:S(2)}) collective-permute-start(f32[4,18,1,128]{3,0,2,1:T(4,128)S(1)} %copy.239), channel_id=1, source_target_pairs={{2,0},{4,2},{6,4},{3,1},{5,3},{7,5},{10,8},{12,10},{14,12},{11,9},... | collective-permute-start | bytes 110600 | tf_op jit(solution)/shard_map/ppermute | solution.py:20
  16.7 5.9 %copy-start.52 = (f32[1,128]{1,0:T(1,128)}, f32[1,128]{1,0:T(1,128)S(1)}, u32[]{:S(2)}) copy-start(f32[1,128]{1,0:T(1,128)S(1)} %collective-permute-done.6) | copy-start | bytes 1540
  16.7 5.9 %copy-start.53 = (f32[1,128]{1,0:T(1,128)}, f32[1,128]{1,0:T(1,128)S(1)}, u32[]{:S(2)}) copy-start(f32[1,128]{1,0:T(1,128)S(1)} %collective-permute-done.7) | copy-start | bytes 1540
  22.6 14.6 %collective-permute-start.4 = (f32[4,18,42,1]{2,0,3,1:T(4,128)S(1)}, f32[4,18,42,1]{2,0,3,1:T(4,128)S(1)}, u32[]{:S(2)}, u32[]{:S(2)}) collective-permute-start(f32[4,18,42,1]{2,0,3,1:T(4,128)S(1)} %copy.212), channel_id=1, source_target_pairs={{0,8},{8,16},{16,24},{1,9},{9,17},{17,25},{2,10},{10,18},{18,26},{... | collective-permute-start | bytes 36296 | tf_op jit(solution)/shard_map/ppermute | solution.py:18
  26.8 11.2 %collective-permute-start.5 = (f32[4,18,42,1]{2,0,3,1:T(4,128)S(1)}, f32[4,18,42,1]{2,0,3,1:T(4,128)S(1)}, u32[]{:S(2)}, u32[]{:S(2)}) collective-permute-start(f32[4,18,42,1]{2,0,3,1:T(4,128)S(1)} %copy.213), channel_id=1, source_target_pairs={{8,0},{16,8},{24,16},{9,1},{17,9},{25,17},{10,2},{18,10},{26,18},{... | collective-permute-start | bytes 36296 | tf_op jit(solution)/shard_map/ppermute | solution.py:20
  30.8 24.7 %collective-permute-start.8 = (f32[42,1]{1,0:T(8,128)}, f32[42,1]{1,0:T(8,128)}, u32[]{:S(2)}, u32[]{:S(2)}) collective-permute-start(f32[42,1]{1,0:T(8,128)} %get-tuple-element.64), channel_id=1, source_target_pairs={{8,0},{16,8},{24,16},{9,1},{17,9},{25,17},{10,2},{18,10},{26,18},{... | collective-permute-start | bytes 512 | tf_op jit(solution)/shard_map/ppermute | solution.py:20
  33.2 22.3 %collective-permute-start.9 = (f32[42,1]{1,0:T(8,128)}, f32[42,1]{1,0:T(8,128)}, u32[]{:S(2)}, u32[]{:S(2)}) collective-permute-start(f32[42,1]{1,0:T(8,128)} %get-tuple-element.65), channel_id=1, source_target_pairs={{0,8},{8,16},{16,24},{1,9},{9,17},{17,25},{2,10},{10,18},{18,26},{... | collective-permute-start | bytes 512 | tf_op jit(solution)/shard_map/ppermute | solution.py:18
  42.6 3.6 %copy-start.2 = (f32[16,40,128]{2,1,0:T(8,128)}, f32[16,40,128]{2,1,0:T(8,128)S(1)}, u32[]{:S(2)}) copy-start(f32[16,40,128]{2,1,0:T(8,128)S(1)} %get-tuple-element.37) | copy-start | bytes 983044
  42.6 3.6 %copy-start.4 = (f32[16,40,128]{2,1,0:T(8,128)}, f32[16,40,128]{2,1,0:T(8,128)S(1)}, u32[]{:S(2)}) copy-start(f32[16,40,128]{2,1,0:T(8,128)S(1)} %get-tuple-element.39) | copy-start | bytes 983044
  42.6 3.6 %copy-start.6 = (f32[16,40,128]{2,1,0:T(8,128)}, f32[16,40,128]{2,1,0:T(8,128)S(1)}, u32[]{:S(2)}) copy-start(f32[16,40,128]{2,1,0:T(8,128)S(1)} %get-tuple-element.41) | copy-start | bytes 983044
  42.6 3.6 %copy-start.8 = (f32[16,40,128]{2,1,0:T(8,128)}, f32[16,40,128]{2,1,0:T(8,128)S(1)}, u32[]{:S(2)}) copy-start(f32[16,40,128]{2,1,0:T(8,128)S(1)} %get-tuple-element.43) | copy-start | bytes 983044
  42.6 3.6 %copy-start.11 = (f32[16,40,128]{2,1,0:T(8,128)}, f32[16,40,128]{2,1,0:T(8,128)S(1)}, u32[]{:S(2)}) copy-start(f32[16,40,128]{2,1,0:T(8,128)S(1)} %get-tuple-element.34) | copy-start | bytes 983044
  42.7 3.6 %copy-start.13 = (f32[16,40,128]{2,1,0:T(8,128)}, f32[16,40,128]{2,1,0:T(8,128)S(1)}, u32[]{:S(2)}) copy-start(f32[16,40,128]{2,1,0:T(8,128)S(1)} %get-tuple-element.35) | copy-start | bytes 983044
  42.9 3.5 %copy-start.46 = (f32[16]{0:T(128)S(1)}, f32[16]{0:T(128)}, u32[]{:S(2)}) copy-start(f32[16]{0:T(128)} %get-tuple-element.93) | copy-start | bytes 196
  56.4 5.9 %collective-permute-start.10 = (f32[1,128]{1,0:T(1,128)S(1)}, f32[1,128]{1,0:T(1,128)S(1)}, u32[]{:S(2)}, u32[]{:S(2)}) collective-permute-start(f32[1,128]{1,0:T(1,128)S(1)} %get-tuple-element.85), channel_id=1, source_target_pairs={{2,0},{4,2},{6,4},{3,1},{5,3},{7,5},{10,8},{12,10},{14,12},{11,9},... | collective-permute-start | bytes 1544 | tf_op jit(solution)/shard_map/ppermute | solution.py:20
  60.8 130.9 %copy-start.3 = (f32[16,40,128]{2,1,0:T(8,128)S(1)}, f32[16,40,128]{2,1,0:T(8,128)}, u32[]{:S(2)}) copy-start(f32[16,40,128]{2,1,0:T(8,128)} %copy-done.2) | copy-start | bytes 983044
  60.8 130.9 %copy-start.5 = (f32[16,40,128]{2,1,0:T(8,128)S(1)}, f32[16,40,128]{2,1,0:T(8,128)}, u32[]{:S(2)}) copy-start(f32[16,40,128]{2,1,0:T(8,128)} %copy-done.4) | copy-start | bytes 983044
  60.8 130.9 %copy-start.7 = (f32[16,40,128]{2,1,0:T(8,128)S(1)}, f32[16,40,128]{2,1,0:T(8,128)}, u32[]{:S(2)}) copy-start(f32[16,40,128]{2,1,0:T(8,128)} %copy-done.6) | copy-start | bytes 983044
  60.8 130.9 %copy-start.9 = (f32[16,40,128]{2,1,0:T(8,128)S(1)}, f32[16,40,128]{2,1,0:T(8,128)}, u32[]{:S(2)}) copy-start(f32[16,40,128]{2,1,0:T(8,128)} %copy-done.8) | copy-start | bytes 983044
  60.8 130.9 %copy-start.25 = (f32[16]{0:T(128)S(1)}, f32[16]{0:T(128)}, u32[]{:S(2)}) copy-start(f32[16]{0:T(128)} %get-tuple-element.86) | copy-start | bytes 196
  60.8 5.6 %collective-permute-start.11 = (f32[1,128]{1,0:T(1,128)S(1)}, f32[1,128]{1,0:T(1,128)S(1)}, u32[]{:S(2)}, u32[]{:S(2)}) collective-permute-start(f32[1,128]{1,0:T(1,128)S(1)} %get-tuple-element.84), channel_id=1, source_target_pairs={{0,2},{2,4},{4,6},{1,3},{3,5},{5,7},{8,10},{10,12},{12,14},{9,11},... | collective-permute-start | bytes 1544 | tf_op jit(solution)/shard_map/ppermute | solution.py:18
  66.5 5.8 %collective-permute-start.12 = (f32[42,1]{1,0:T(8,128)S(1)}, f32[42,1]{1,0:T(8,128)S(1)}, u32[]{:S(2)}, u32[]{:S(2)}) collective-permute-start(f32[42,1]{1,0:T(8,128)S(1)} %get-tuple-element.62), channel_id=1, source_target_pairs={{8,0},{16,8},{24,16},{9,1},{17,9},{25,17},{10,2},{18,10},{26,18},{... | collective-permute-start | bytes 512 | tf_op jit(solution)/shard_map/ppermute | solution.py:20
  69.3 6.6 %collective-permute-start.13 = (f32[42,1]{1,0:T(8,128)S(1)}, f32[42,1]{1,0:T(8,128)S(1)}, u32[]{:S(2)}, u32[]{:S(2)}) collective-permute-start(f32[42,1]{1,0:T(8,128)S(1)} %get-tuple-element.63), channel_id=1, source_target_pairs={{0,8},{8,16},{16,24},{1,9},{9,17},{17,25},{2,10},{10,18},{18,26},{... | collective-permute-start | bytes 512 | tf_op jit(solution)/shard_map/ppermute | solution.py:18
  76.0 5.2 %collective-permute-start.14 = (f32[1,128]{1,0:T(1,128)S(1)}, f32[1,128]{1,0:T(1,128)S(1)}, u32[]{:S(2)}, u32[]{:S(2)}) collective-permute-start(f32[1,128]{1,0:T(1,128)S(1)} %get-tuple-element.83), channel_id=1, source_target_pairs={{2,0},{4,2},{6,4},{3,1},{5,3},{7,5},{10,8},{12,10},{14,12},{11,9},... | collective-permute-start | bytes 1544 | tf_op jit(solution)/shard_map/ppermute | solution.py:20
  79.9 5.5 %collective-permute-start.15 = (f32[1,128]{1,0:T(1,128)S(1)}, f32[1,128]{1,0:T(1,128)S(1)}, u32[]{:S(2)}, u32[]{:S(2)}) collective-permute-start(f32[1,128]{1,0:T(1,128)S(1)} %get-tuple-element.82), channel_id=1, source_target_pairs={{0,2},{2,4},{4,6},{1,3},{3,5},{5,7},{8,10},{10,12},{12,14},{9,11},... | collective-permute-start | bytes 1544 | tf_op jit(solution)/shard_map/ppermute | solution.py:18
  85.5 5.8 %collective-permute-start.16 = (f32[42,1]{1,0:T(8,128)S(1)}, f32[42,1]{1,0:T(8,128)S(1)}, u32[]{:S(2)}, u32[]{:S(2)}) collective-permute-start(f32[42,1]{1,0:T(8,128)S(1)} %get-tuple-element.60), channel_id=1, source_target_pairs={{8,0},{16,8},{24,16},{9,1},{17,9},{25,17},{10,2},{18,10},{26,18},{... | collective-permute-start | bytes 512 | tf_op jit(solution)/shard_map/ppermute | solution.py:20
  87.4 6.6 %collective-permute-start.17 = (f32[42,1]{1,0:T(8,128)S(1)}, f32[42,1]{1,0:T(8,128)S(1)}, u32[]{:S(2)}, u32[]{:S(2)}) collective-permute-start(f32[42,1]{1,0:T(8,128)S(1)} %get-tuple-element.61), channel_id=1, source_target_pairs={{0,8},{8,16},{16,24},{1,9},{9,17},{17,25},{2,10},{10,18},{18,26},{... | collective-permute-start | bytes 512 | tf_op jit(solution)/shard_map/ppermute | solution.py:18
  94.1 3.7 %collective-permute-start.18 = (f32[1,128]{1,0:T(1,128)S(1)}, f32[1,128]{1,0:T(1,128)S(1)}, u32[]{:S(2)}, u32[]{:S(2)}) collective-permute-start(f32[1,128]{1,0:T(1,128)S(1)} %get-tuple-element.81), channel_id=1, source_target_pairs={{2,0},{4,2},{6,4},{3,1},{5,3},{7,5},{10,8},{12,10},{14,12},{11,9},... | collective-permute-start | bytes 1544 | tf_op jit(solution)/shard_map/ppermute | solution.py:20
  96.5 5.5 %collective-permute-start.19 = (f32[1,128]{1,0:T(1,128)S(1)}, f32[1,128]{1,0:T(1,128)S(1)}, u32[]{:S(2)}, u32[]{:S(2)}) collective-permute-start(f32[1,128]{1,0:T(1,128)S(1)} %get-tuple-element.80), channel_id=1, source_target_pairs={{0,2},{2,4},{4,6},{1,3},{3,5},{5,7},{8,10},{10,12},{12,14},{9,11},... | collective-permute-start | bytes 1544 | tf_op jit(solution)/shard_map/ppermute | solution.py:18
  102.0 5.8 %collective-permute-start.20 = (f32[42,1]{1,0:T(8,128)S(1)}, f32[42,1]{1,0:T(8,128)S(1)}, u32[]{:S(2)}, u32[]{:S(2)}) collective-permute-start(f32[42,1]{1,0:T(8,128)S(1)} %get-tuple-element.58), channel_id=1, source_target_pairs={{8,0},{16,8},{24,16},{9,1},{17,9},{25,17},{10,2},{18,10},{26,18},{... | collective-permute-start | bytes 512 | tf_op jit(solution)/shard_map/ppermute | solution.py:20
  104.0 6.6 %collective-permute-start.21 = (f32[42,1]{1,0:T(8,128)S(1)}, f32[42,1]{1,0:T(8,128)S(1)}, u32[]{:S(2)}, u32[]{:S(2)}) collective-permute-start(f32[42,1]{1,0:T(8,128)S(1)} %get-tuple-element.59), channel_id=1, source_target_pairs={{0,8},{8,16},{16,24},{1,9},{9,17},{17,25},{2,10},{10,18},{18,26},{... | collective-permute-start | bytes 512 | tf_op jit(solution)/shard_map/ppermute | solution.py:18
  110.7 3.2 %collective-permute-start.22 = (f32[1,128]{1,0:T(1,128)S(1)}, f32[1,128]{1,0:T(1,128)S(1)}, u32[]{:S(2)}, u32[]{:S(2)}) collective-permute-start(f32[1,128]{1,0:T(1,128)S(1)} %get-tuple-element.79), channel_id=1, source_target_pairs={{2,0},{4,2},{6,4},{3,1},{5,3},{7,5},{10,8},{12,10},{14,12},{11,9},... | collective-permute-start | bytes 1544 | tf_op jit(solution)/shard_map/ppermute | solution.py:20
  112.6 5.5 %collective-permute-start.23 = (f32[1,128]{1,0:T(1,128)S(1)}, f32[1,128]{1,0:T(1,128)S(1)}, u32[]{:S(2)}, u32[]{:S(2)}) collective-permute-start(f32[1,128]{1,0:T(1,128)S(1)} %get-tuple-element.78), channel_id=1, source_target_pairs={{0,2},{2,4},{4,6},{1,3},{3,5},{5,7},{8,10},{10,12},{12,14},{9,11},... | collective-permute-start | bytes 1544 | tf_op jit(solution)/shard_map/ppermute | solution.py:18
  118.2 5.8 %collective-permute-start.24 = (f32[42,1]{1,0:T(8,128)S(1)}, f32[42,1]{1,0:T(8,128)S(1)}, u32[]{:S(2)}, u32[]{:S(2)}) collective-permute-start(f32[42,1]{1,0:T(8,128)S(1)} %get-tuple-element.56), channel_id=1, source_target_pairs={{8,0},{16,8},{24,16},{9,1},{17,9},{25,17},{10,2},{18,10},{26,18},{... | collective-permute-start | bytes 512 | tf_op jit(solution)/shard_map/ppermute | solution.py:20
  120.1 6.6 %collective-permute-start.25 = (f32[42,1]{1,0:T(8,128)S(1)}, f32[42,1]{1,0:T(8,128)S(1)}, u32[]{:S(2)}, u32[]{:S(2)}) collective-permute-start(f32[42,1]{1,0:T(8,128)S(1)} %get-tuple-element.57), channel_id=1, source_target_pairs={{0,8},{8,16},{16,24},{1,9},{9,17},{17,25},{2,10},{10,18},{18,26},{... | collective-permute-start | bytes 512 | tf_op jit(solution)/shard_map/ppermute | solution.py:18
  126.8 3.3 %collective-permute-start.26 = (f32[1,128]{1,0:T(1,128)S(1)}, f32[1,128]{1,0:T(1,128)S(1)}, u32[]{:S(2)}, u32[]{:S(2)}) collective-permute-start(f32[1,128]{1,0:T(1,128)S(1)} %get-tuple-element.77), channel_id=1, source_target_pairs={{2,0},{4,2},{6,4},{3,1},{5,3},{7,5},{10,8},{12,10},{14,12},{11,9},... | collective-permute-start | bytes 1544 | tf_op jit(solution)/shard_map/ppermute | solution.py:20
  128.8 5.5 %collective-permute-start.27 = (f32[1,128]{1,0:T(1,128)S(1)}, f32[1,128]{1,0:T(1,128)S(1)}, u32[]{:S(2)}, u32[]{:S(2)}) collective-permute-start(f32[1,128]{1,0:T(1,128)S(1)} %get-tuple-element.76), channel_id=1, source_target_pairs={{0,2},{2,4},{4,6},{1,3},{3,5},{5,7},{8,10},{10,12},{12,14},{9,11},... | collective-permute-start | bytes 1544 | tf_op jit(solution)/shard_map/ppermute | solution.py:18
  134.4 5.8 %collective-permute-start.28 = (f32[42,1]{1,0:T(8,128)S(1)}, f32[42,1]{1,0:T(8,128)S(1)}, u32[]{:S(2)}, u32[]{:S(2)}) collective-permute-start(f32[42,1]{1,0:T(8,128)S(1)} %get-tuple-element.54), channel_id=1, source_target_pairs={{8,0},{16,8},{24,16},{9,1},{17,9},{25,17},{10,2},{18,10},{26,18},{... | collective-permute-start | bytes 512 | tf_op jit(solution)/shard_map/ppermute | solution.py:20
  136.3 6.6 %collective-permute-start.29 = (f32[42,1]{1,0:T(8,128)S(1)}, f32[42,1]{1,0:T(8,128)S(1)}, u32[]{:S(2)}, u32[]{:S(2)}) collective-permute-start(f32[42,1]{1,0:T(8,128)S(1)} %get-tuple-element.55), channel_id=1, source_target_pairs={{0,8},{8,16},{16,24},{1,9},{9,17},{17,25},{2,10},{10,18},{18,26},{... | collective-permute-start | bytes 512 | tf_op jit(solution)/shard_map/ppermute | solution.py:18
  143.0 3.3 %collective-permute-start.30 = (f32[1,128]{1,0:T(1,128)S(1)}, f32[1,128]{1,0:T(1,128)S(1)}, u32[]{:S(2)}, u32[]{:S(2)}) collective-permute-start(f32[1,128]{1,0:T(1,128)S(1)} %get-tuple-element.75), channel_id=1, source_target_pairs={{2,0},{4,2},{6,4},{3,1},{5,3},{7,5},{10,8},{12,10},{14,12},{11,9},... | collective-permute-start | bytes 1544 | tf_op jit(solution)/shard_map/ppermute | solution.py:20
  145.0 5.5 %collective-permute-start.31 = (f32[1,128]{1,0:T(1,128)S(1)}, f32[1,128]{1,0:T(1,128)S(1)}, u32[]{:S(2)}, u32[]{:S(2)}) collective-permute-start(f32[1,128]{1,0:T(1,128)S(1)} %get-tuple-element.74), channel_id=1, source_target_pairs={{0,2},{2,4},{4,6},{1,3},{3,5},{5,7},{8,10},{10,12},{12,14},{9,11},... | collective-permute-start | bytes 1544 | tf_op jit(solution)/shard_map/ppermute | solution.py:18
  150.5 5.8 %collective-permute-start.32 = (f32[42,1]{1,0:T(8,128)S(1)}, f32[42,1]{1,0:T(8,128)S(1)}, u32[]{:S(2)}, u32[]{:S(2)}) collective-permute-start(f32[42,1]{1,0:T(8,128)S(1)} %get-tuple-element.52), channel_id=1, source_target_pairs={{8,0},{16,8},{24,16},{9,1},{17,9},{25,17},{10,2},{18,10},{26,18},{... | collective-permute-start | bytes 512 | tf_op jit(solution)/shard_map/ppermute | solution.py:20
  152.5 6.6 %collective-permute-start.33 = (f32[42,1]{1,0:T(8,128)S(1)}, f32[42,1]{1,0:T(8,128)S(1)}, u32[]{:S(2)}, u32[]{:S(2)}) collective-permute-start(f32[42,1]{1,0:T(8,128)S(1)} %get-tuple-element.53), channel_id=1, source_target_pairs={{0,8},{8,16},{16,24},{1,9},{9,17},{17,25},{2,10},{10,18},{18,26},{... | collective-permute-start | bytes 512 | tf_op jit(solution)/shard_map/ppermute | solution.py:18
  159.2 3.2 %collective-permute-start.34 = (f32[1,128]{1,0:T(1,128)S(1)}, f32[1,128]{1,0:T(1,128)S(1)}, u32[]{:S(2)}, u32[]{:S(2)}) collective-permute-start(f32[1,128]{1,0:T(1,128)S(1)} %get-tuple-element.73), channel_id=1, source_target_pairs={{2,0},{4,2},{6,4},{3,1},{5,3},{7,5},{10,8},{12,10},{14,12},{11,9},... | collective-permute-start | bytes 1544 | tf_op jit(solution)/shard_map/ppermute | solution.py:20
  161.1 5.5 %collective-permute-start.35 = (f32[1,128]{1,0:T(1,128)S(1)}, f32[1,128]{1,0:T(1,128)S(1)}, u32[]{:S(2)}, u32[]{:S(2)}) collective-permute-start(f32[1,128]{1,0:T(1,128)S(1)} %get-tuple-element.72), channel_id=1, source_target_pairs={{0,2},{2,4},{4,6},{1,3},{3,5},{5,7},{8,10},{10,12},{12,14},{9,11},... | collective-permute-start | bytes 1544 | tf_op jit(solution)/shard_map/ppermute | solution.py:18
  166.6 25.4 %copy-start.20 = (f32[16]{0:T(128)S(1)}, f32[16]{0:T(128)}, u32[]{:S(2)}) copy-start(f32[16]{0:T(128)} %copy-done.19) | copy-start | bytes 196
  166.6 25.4 %copy-start.23 = (f32[16]{0:T(128)S(1)}, f32[16]{0:T(128)}, u32[]{:S(2)}) copy-start(f32[16]{0:T(128)} %get-tuple-element.92) | copy-start | bytes 196
  166.7 5.8 %collective-permute-start.36 = (f32[42,1]{1,0:T(8,128)S(1)}, f32[42,1]{1,0:T(8,128)S(1)}, u32[]{:S(2)}, u32[]{:S(2)}) collective-permute-start(f32[42,1]{1,0:T(8,128)S(1)} %get-tuple-element.50), channel_id=1, source_target_pairs={{8,0},{16,8},{24,16},{9,1},{17,9},{25,17},{10,2},{18,10},{26,18},{... | collective-permute-start | bytes 512 | tf_op jit(solution)/shard_map/ppermute | solution.py:20
  168.6 6.6 %collective-permute-start.37 = (f32[42,1]{1,0:T(8,128)S(1)}, f32[42,1]{1,0:T(8,128)S(1)}, u32[]{:S(2)}, u32[]{:S(2)}) collective-permute-start(f32[42,1]{1,0:T(8,128)S(1)} %get-tuple-element.51), channel_id=1, source_target_pairs={{0,8},{8,16},{16,24},{1,9},{9,17},{17,25},{2,10},{10,18},{18,26},{... | collective-permute-start | bytes 512 | tf_op jit(solution)/shard_map/ppermute | solution.py:18
  175.3 16.9 %copy-start.15 = (f32[40,128]{1,0:T(8,128)}, f32[40,128]{1,0:T(8,128)S(1)}, u32[]{:S(2)}) copy-start(f32[40,128]{1,0:T(8,128)S(1)} %fusion.73) | copy-start | bytes 61444
  175.4 3.5 %collective-permute-start.38 = (f32[1,128]{1,0:T(1,128)S(1)}, f32[1,128]{1,0:T(1,128)S(1)}, u32[]{:S(2)}, u32[]{:S(2)}) collective-permute-start(f32[1,128]{1,0:T(1,128)S(1)} %get-tuple-element.71), channel_id=1, source_target_pairs={{2,0},{4,2},{6,4},{3,1},{5,3},{7,5},{10,8},{12,10},{14,12},{11,9},... | collective-permute-start | bytes 1544 | tf_op jit(solution)/shard_map/ppermute | solution.py:20
  177.5 5.5 %collective-permute-start.39 = (f32[1,128]{1,0:T(1,128)S(1)}, f32[1,128]{1,0:T(1,128)S(1)}, u32[]{:S(2)}, u32[]{:S(2)}) collective-permute-start(f32[1,128]{1,0:T(1,128)S(1)} %get-tuple-element.70), channel_id=1, source_target_pairs={{0,2},{2,4},{4,6},{1,3},{3,5},{5,7},{8,10},{10,12},{12,14},{9,11},... | collective-permute-start | bytes 1544 | tf_op jit(solution)/shard_map/ppermute | solution.py:18
  183.1 6.1 %collective-permute-start.40 = (f32[42,1]{1,0:T(8,128)S(1)}, f32[42,1]{1,0:T(8,128)S(1)}, u32[]{:S(2)}, u32[]{:S(2)}) collective-permute-start(f32[42,1]{1,0:T(8,128)S(1)} %get-tuple-element.48), channel_id=1, source_target_pairs={{8,0},{16,8},{24,16},{9,1},{17,9},{25,17},{10,2},{18,10},{26,18},{... | collective-permute-start | bytes 512 | tf_op jit(solution)/shard_map/ppermute | solution.py:20
  185.0 6.6 %collective-permute-start.41 = (f32[42,1]{1,0:T(8,128)S(1)}, f32[42,1]{1,0:T(8,128)S(1)}, u32[]{:S(2)}, u32[]{:S(2)}) collective-permute-start(f32[42,1]{1,0:T(8,128)S(1)} %get-tuple-element.49), channel_id=1, source_target_pairs={{0,8},{8,16},{16,24},{1,9},{9,17},{17,25},{2,10},{10,18},{18,26},{... | collective-permute-start | bytes 512 | tf_op jit(solution)/shard_map/ppermute | solution.py:18
  (33 other events, 43.4 us)
